TPU v7x, 128 devices: a whole 4x4x4 slice. The times are simulated.
128 devices in a mesh: gx: 8 (over z, core), gy: 16 (over y, x).
Axes of the slice: x: 4, y: 4, z: 4, core: 2. Of those that a mesh axis runs over, the one named last changes fastest.
Arguments:
- hidden: bfloat16 [8, 16384], replicated, may hold values from -6 to 6
- norm_gain: float32 [16384], replicated, may hold values from 0.5 to 1.5
- q_codes: int32 [16384, 8192], P('gx', 'gy'), may hold values from 0 to 255, as said below
- q_absmax: float32 [256, 16384], P('gx', 'gy'), may hold values from 0.0046875 to 0.046875
- kv_codes: int32 [16384, 1024], P('gx', 'gy'), may hold values from 0 to 255
- kv_absmax: float32 [256, 2048], P('gx', 'gy'), may hold values from 0.015625 to 0.15625
- o_codes: int32 [16384, 8192], P('gx', 'gy'), may hold values from 0 to 255, as said below
- o_absmax: float32 [256, 16384], P('gx', 'gy'), may hold values from 0.0046875 to 0.046875
- q_down: bfloat16 [8, 16384, 16], P(None, 'gx'), may hold values from -0.140625 to 0.140625
- q_up: bfloat16 [8, 16, 16384], P(None, None, 'gy'), may hold values from -1.5 to 1.5
- q_magnitude: float32 [8, 16384], P(None, 'gy'), may hold values from 0.25 to 1.75
- o_down: bfloat16 [8, 16384, 16], P(None, 'gx'), may hold values from -0.140625 to 0.140625
- o_up: bfloat16 [8, 16, 16384], P(None, None, 'gy'), may hold values from -1.5 to 1.5
- o_magnitude: float32 [8, 16384], P(None, 'gy'), may hold values from 0.25 to 1.75
- tenant: int32 [8], replicated, may hold values from 0 to 7
- lengths: int32 [8], replicated, may hold values from 1 to 24576, as said below
- page_table: int32 [8, 96], replicated, may hold values from 0 to 639, as said below
- kv_cache: bfloat16 [640, 2, 256, 1024], P(('gx', 'gy')), may hold values from -1080 to 1080, as said below
Outputs:
- layer_out: bfloat16 [8, 16384], P('gx', 'gy')
Inputs may be any that keep to these rules, and one draw needn't show every extreme that they name: `q_codes`: each word holds two 4-bit codes: word % 16 for the even column and word // 16 for the odd one. `kv_codes`: each word holds two 4-bit codes: word % 16 for the even column and word // 16 for the odd one. `o_codes`: each word holds two 4-bit codes: word % 16 for the even column and word // 16 for the odd one. `lengths`: one row holds exactly 24576 tokens; every other row fewer than 16384. `page_table`: for j below ceil(lengths[r] / 256), entry [r, j] is the global slot of page j of row r: device index along gx+gy times 5 plus the slot on that device; no slot holds two pages; other entries are 0 and are not read. On every device the used slots are its first ones; no device holds more than 5 pages and some device holds exactly 5. `kv_cache`: row d * 5 + s holds slot s of device d; unused slots hold finite values.
All inputs are finite; a program needn't handle non-finite values.
Results may differ from a plain program's by a relative error of at most 0.01.
The roundings to bfloat16 on the way count: a program that leaves them out, or rounds other values in their place, can miss the bound.
Values may be sent and summed in bfloat16 or wider, within the bound.
A program may use at most 192 MiB of HBM per device.

v0:
```python
import functools
import math

import jax
import jax.numpy as jnp
from jax import lax
from jax.sharding import Mesh
from jax.sharding import PartitionSpec as P

HEADS = 128
KV_HEADS = 8
HEAD_DIM = 128
TENANTS = 8
QBLOCK = 64
PAGE = 256
GX = ("gx_0", "gx_1")
GY = ("gy_0", "gy_1")
GX_GY = ("gx_0", "gx_1", "gy_0", "gy_1")


NF4_LEVELS = (
    -1.0,
    -0.6961928009986877,
    -0.5250730514526367,
    -0.39491748809814453,
    -0.28444138169288635,
    -0.18477343022823334,
    -0.09105003625154495,
    0.0,
    0.07958029955625534,
    0.16093020141124725,
    0.24611230194568634,
    0.33791524171829224,
    0.44070982933044434,
    0.5626170039176941,
    0.7229568362236023,
    1.0,
)
NORM_EPS = 1e-05
NEG_FILL = -1e30
ROPE_BASE = 500000.0
PRECISE = lax.Precision.HIGHEST


def cut_along(x, dim, length):
    shape = x.shape
    blocks = x.reshape(*shape[:dim], length, shape[dim] // length, *shape[dim + 1 :])
    return jnp.moveaxis(blocks, dim, 0)


def sum_at_owner(x, axis, dim):
    length = lax.axis_size(axis)
    blocks = lax.all_to_all(cut_along(x, dim, length), axis, 0, 0, tiled=True)
    return jnp.sum(blocks, axis=0)


def swapped(value, axis, bit):
    mask = 2**bit
    pairs = [(source, source ^ mask) for source in range(lax.axis_size(axis))]
    return lax.ppermute(value, axis, pairs)


def by_axis(x, axes):
    return functools.reduce(lax.pmax, axes, x)


def sent_together(arrays, axis, dim, along):
    columns = [a.reshape(*a.shape[:along], -1) for a in arrays]
    both = jnp.concatenate(columns, axis=along)
    whole, at, outs = (lax.psum_scatter(both, axis, scatter_dimension=dim, tiled=True), 0, [])
    for a, column in zip(arrays, columns):
        piece = whole[..., at : at + column.shape[along]]
        outs.append(piece.reshape(*piece.shape[:along], *a.shape[along:]))
        at += column.shape[along]
    return tuple(outs)


def from_everyone(x, axis):
    copies = jnp.broadcast_to(x, (lax.axis_size(axis), *x.shape))
    return lax.all_to_all(copies, axis, split_axis=0, concat_axis=0, tiled=True)


def of_everyone(x, axis):
    return from_everyone(x, axis).sum(axis=0)


def together(arrays, axis):
    ends = [0]
    for a in arrays:
        ends.append(ends[-1] + a.size)
    total = of_everyone(jnp.concatenate([a.ravel() for a in arrays]), axis)
    return tuple((total[b:e].reshape(a.shape) for a, b, e in zip(arrays, ends, ends[1:])))


def nf4_value(code_array):
    level_list = [jnp.float32(level_value) for level_value in NF4_LEVELS]
    for bit_place in range(4):
        bit_set = code_array // 2**bit_place % 2 == 1
        level_list = [
            jnp.where(bit_set, level_list[2 * pair_index + 1], level_list[2 * pair_index])
            for pair_index in range(len(level_list) // 2)
        ]
    return level_list[0]


def dequantize(packed, absmax):
    low_levels = nf4_value(packed % 16)
    high_levels = nf4_value(packed // 16)
    in_count, half_cols = packed.shape
    levels = jnp.stack([low_levels, high_levels], axis=-1).reshape(
        in_count // QBLOCK, QBLOCK, 2 * half_cols
    )
    return (levels * absmax[:, None, :]).reshape(in_count, 2 * half_cols).astype(jnp.bfloat16)


def rotate(values, positions):
    row_count = values.shape[0]
    half_dim = HEAD_DIM // 2
    frequency = ROPE_BASE ** (-2.0 * jnp.arange(half_dim, dtype=jnp.float32) / HEAD_DIM)
    angles = positions.astype(jnp.float32)[:, None, None] * frequency[None, None, :]
    cosine = jnp.cos(angles)
    sine_part = jnp.sin(angles)
    head_view = values.reshape(row_count, -1, HEAD_DIM)
    front_half = head_view[..., :half_dim]
    back_half = head_view[..., half_dim:]
    turned = jnp.concatenate(
        [front_half * cosine - back_half * sine_part, back_half * cosine + front_half * sine_part],
        axis=-1,
    )
    return turned.reshape(row_count, -1)


def dora_terms(weight, down):
    cross_terms = jnp.einsum("tdk,dc->tkc", down, weight, preferred_element_type=jnp.float32)
    weight_float = weight.astype(jnp.float32)
    squares = jnp.sum(weight_float * weight_float, axis=0)[None, None, :]
    gram_matrix = jnp.einsum("tdk,tdl->tkl", down, down, preferred_element_type=jnp.float32)
    return (cross_terms, squares, gram_matrix)


def column_scale(cross_terms, squares, gram_matrix, up, magnitude):
    up_float = up.astype(jnp.float32)
    quadratic = jnp.einsum("tkc,tkl,tlc->tc", up_float, gram_matrix, up_float, precision=PRECISE)
    linear = jnp.sum(up_float * cross_terms, axis=1)
    return magnitude * lax.rsqrt(squares[0] + 2.0 * linear + quadratic)


def adapted(inputs, weight, down, up, selector):
    product = jnp.dot(inputs, weight, preferred_element_type=jnp.float32)
    middle = (
        jnp.einsum("rd,tdk->rtk", inputs, down, preferred_element_type=jnp.float32)
        * selector[:, :, None]
    )
    adapter_part = jnp.dot(
        middle.reshape(middle.shape[0], -1),
        up.astype(jnp.float32).reshape(-1, up.shape[2]),
        precision=PRECISE,
    )
    return product + adapter_part


def slot_info(page_table, lengths, device, slot_count):
    row_count, page_limit = page_table.shape
    page_need = (lengths + PAGE - 1) // PAGE
    page_numbers = jnp.arange(page_limit, dtype=jnp.int32)
    live_mask = page_numbers[None, :] < page_need[:, None]
    wanted = device * slot_count + jnp.arange(slot_count, dtype=jnp.int32)
    hits = ((page_table[None, :, :] == wanted[:, None, None]) & live_mask[None, :, :]).astype(
        jnp.int32
    )
    owner_row = jnp.sum(hits * jnp.arange(row_count, dtype=jnp.int32)[None, :, None], axis=(1, 2))
    remaining = jnp.clip(lengths[:, None] - page_numbers[None, :] * PAGE, 0, PAGE)
    filled = jnp.sum(hits * remaining[None, :, :], axis=(1, 2))
    return (owner_row, filled, jnp.sum(hits))


def attend_pages(
    pages, first_slot, stride, owner_row, filled, page_count, query_heads, carry_state
):
    inv_root = 1.0 / math.sqrt(HEAD_DIM)

    def visit_page(position, carry):
        best_score, denominator, numerator = carry
        slot_index = first_slot + stride * position
        page_block = lax.dynamic_index_in_dim(pages, slot_index, 0, keepdims=False)
        row_id = lax.dynamic_index_in_dim(owner_row, position, 0, keepdims=False)
        token_count = lax.dynamic_index_in_dim(filled, position, 0, keepdims=False)
        key_rows = page_block[0].reshape(PAGE, KV_HEADS, HEAD_DIM)
        value_rows = page_block[1].reshape(PAGE, KV_HEADS, HEAD_DIM)
        query_row = lax.dynamic_index_in_dim(query_heads, row_id, 0, keepdims=False)
        scores = (
            jnp.einsum("ghd,tgd->ght", query_row, key_rows, preferred_element_type=jnp.float32)
            * inv_root
        )
        inside = jnp.arange(PAGE, dtype=jnp.int32) < token_count
        scores = jnp.where(inside[None, None, :], scores, NEG_FILL)
        page_peak = jnp.max(scores, axis=-1)
        weights = jnp.where(inside[None, None, :], jnp.exp(scores - page_peak[..., None]), 0.0)
        page_total = jnp.sum(weights, axis=-1).reshape(HEADS)
        page_values = jnp.einsum(
            "ght,tgd->ghd", weights, value_rows.astype(jnp.float32), precision=PRECISE
        ).reshape(HEADS, HEAD_DIM)
        page_peak = page_peak.reshape(HEADS)
        old_peak = lax.dynamic_index_in_dim(best_score, row_id, 0, keepdims=False)
        old_total = lax.dynamic_index_in_dim(denominator, row_id, 0, keepdims=False)
        old_values = lax.dynamic_index_in_dim(numerator, row_id, 0, keepdims=False)
        new_peak = jnp.maximum(old_peak, page_peak)
        keep_factor = jnp.exp(old_peak - new_peak)
        take_factor = jnp.exp(page_peak - new_peak)
        best_score = lax.dynamic_update_index_in_dim(best_score, new_peak, row_id, 0)
        denominator = lax.dynamic_update_index_in_dim(
            denominator, old_total * keep_factor + page_total * take_factor, row_id, 0
        )
        merged_values = old_values * keep_factor[:, None] + page_values * take_factor[:, None]
        numerator = lax.dynamic_update_index_in_dim(numerator, merged_values, row_id, 0)
        return (best_score, denominator, numerator)

    return lax.fori_loop(0, page_count, visit_page, carry_state)


def local(
    hidden,
    norm_gain,
    q_codes,
    q_absmax,
    kv_codes,
    kv_absmax,
    o_codes,
    o_absmax,
    q_down,
    q_up,
    q_magnitude,
    o_down,
    o_up,
    o_magnitude,
    tenant,
    lengths,
    page_table,
    kv_cache,
):
    row_count = hidden.shape[0]
    row_x = lax.axis_index(GX)
    col_y = lax.axis_index(GY)
    size_x = lax.axis_size(GX)
    size_y = lax.axis_size(GY)
    group = HEADS // KV_HEADS
    states = hidden.astype(jnp.float32)
    mean_square = jnp.mean(states * states, axis=1, keepdims=True)
    normed = (states * lax.rsqrt(mean_square + NORM_EPS) * norm_gain[None, :]).astype(jnp.bfloat16)
    in_width = q_codes.shape[0]
    local_in = lax.dynamic_slice_in_dim(normed, row_x * in_width, in_width, 1)
    onehot = (tenant[:, None] == jnp.arange(TENANTS, dtype=jnp.int32)[None, :]).astype(jnp.float32)
    w_query = dequantize(q_codes, q_absmax)
    w_keyval = dequantize(kv_codes, kv_absmax)
    w_output = dequantize(o_codes, o_absmax)
    query_part = adapted(local_in, w_query, q_down, q_up, onehot)
    keyval_part = jnp.dot(local_in, w_keyval, preferred_element_type=jnp.float32)
    q_cross, q_squares, q_gram = dora_terms(w_query, q_down)
    o_cross, o_squares, o_gram = dora_terms(w_output, o_down)
    query_sum, keyval_sum, q_gram, o_gram = lax.psum((query_part, keyval_part, q_gram, o_gram), GX)
    q_cross, q_squares, o_cross, o_squares = (
        sum_at_owner(q_cross, GX, 2),
        sum_at_owner(q_squares, GX, 2),
        sum_at_owner(o_cross, GX, 2),
        sum_at_owner(o_squares, GX, 2),
    )
    q_share = q_cross.shape[2]
    o_share = o_cross.shape[2]
    q_up_share = lax.dynamic_slice_in_dim(q_up, row_x * q_share, q_share, 2)
    q_magnitude_share = lax.dynamic_slice_in_dim(q_magnitude, row_x * q_share, q_share, 1)
    o_up_share = lax.dynamic_slice_in_dim(o_up, row_x * o_share, o_share, 2)
    o_magnitude_share = lax.dynamic_slice_in_dim(o_magnitude, row_x * o_share, o_share, 1)
    q_scale_share = column_scale(q_cross, q_squares, q_gram, q_up_share, q_magnitude_share)
    o_scale_share = column_scale(o_cross, o_squares, o_gram, o_up_share, o_magnitude_share)
    q_scale, out_scale = (
        lax.all_gather(q_scale_share, GX, axis=1, tiled=True),
        lax.all_gather(o_scale_share, GX, axis=1, tiled=True),
    )
    row_scale = jnp.dot(onehot, q_scale, precision=PRECISE)
    query_local = rotate(query_sum * row_scale, lengths).astype(jnp.bfloat16)
    head_blocks = keyval_sum.shape[1] // HEAD_DIM
    block_ids = col_y * head_blocks + jnp.arange(head_blocks, dtype=jnp.int32)
    key_block = jnp.repeat(block_ids < KV_HEADS, HEAD_DIM)
    keyval_local = jnp.where(key_block[None, :], rotate(keyval_sum, lengths), keyval_sum).astype(
        jnp.bfloat16
    )
    query_full, keyval_full = (
        lax.all_gather(query_local, GY, axis=1, tiled=True),
        lax.all_gather(keyval_local, GY, axis=1, tiled=True),
    )
    query_heads = query_full.reshape(row_count, KV_HEADS, group, HEAD_DIM)
    key_width = KV_HEADS * HEAD_DIM
    new_keys = keyval_full[:, :key_width].reshape(row_count, KV_HEADS, HEAD_DIM)
    new_values = keyval_full[:, key_width:].reshape(row_count, KV_HEADS, HEAD_DIM)
    inv_root = 1.0 / math.sqrt(HEAD_DIM)
    self_score = (
        jnp.einsum(
            "rghd,rgd->rgh", query_heads, new_keys, preferred_element_type=jnp.float32
        ).reshape(row_count, HEADS)
        * inv_root
    )
    slot_count = kv_cache.shape[0]
    device = row_x * size_y + col_y
    owner_row, filled, page_count = slot_info(page_table, lengths, device, slot_count)
    carry_state = (
        jnp.full((row_count, HEADS), NEG_FILL, jnp.float32),
        jnp.zeros((row_count, HEADS), jnp.float32),
        jnp.zeros((row_count, HEADS, HEAD_DIM), jnp.float32),
    )
    partner = row_x * size_y + jnp.bitwise_xor(col_y, 1)
    partner_rows, partner_filled, partner_count = slot_info(
        page_table, lengths, partner, slot_count
    )
    sent_pages = kv_cache[1::2]
    received = swapped(sent_pages, GY, 0)
    carry_state = attend_pages(
        kv_cache,
        0,
        2,
        owner_row[0::2],
        filled[0::2],
        (page_count + 1) // 2,
        query_heads,
        carry_state,
    )
    carry_state = attend_pages(
        received,
        0,
        1,
        partner_rows[1::2],
        partner_filled[1::2],
        partner_count // 2,
        query_heads,
        carry_state,
    )
    best_score, denominator, numerator = carry_state
    head_width = HEADS // size_x
    head_start = row_x * head_width
    own_self = lax.dynamic_slice_in_dim(self_score, head_start, head_width, 1)
    head_values = lax.dynamic_slice_in_dim(
        jnp.repeat(new_values.astype(jnp.float32), group, axis=1), head_start, head_width, 1
    )
    peak_score = by_axis(jnp.maximum(best_score, self_score), GX_GY)
    factor = jnp.exp(best_score - peak_score)
    shares = sent_together((numerator * factor[..., None], denominator * factor), GX, 1, 2)
    numerator_part, denominator_part = together((shares[0], shares[1]), GY)
    own_peak = lax.dynamic_slice_in_dim(peak_score, head_start, head_width, 1)
    own_weight = jnp.exp(own_self - own_peak)
    denominator_part = denominator_part + own_weight
    numerator_part = numerator_part + own_weight[..., None] * head_values
    attended = (
        (numerator_part / denominator_part[..., None])
        .reshape(row_count, head_width * HEAD_DIM)
        .astype(jnp.bfloat16)
    )
    own_rows = row_count // size_x
    out_cols = w_output.shape[1]
    out_sum = sum_at_owner(adapted(attended, w_output, o_down, o_up, onehot), GX, 0)
    my_select = lax.dynamic_slice_in_dim(onehot, row_x * own_rows, own_rows, 0)
    residual = lax.dynamic_slice(states, (row_x * own_rows, col_y * out_cols), (own_rows, out_cols))
    layer_out = residual + out_sum * jnp.dot(my_select, out_scale, precision=PRECISE)
    return layer_out.astype(jnp.bfloat16)


def solution(mesh):
    split = Mesh(mesh.devices.reshape(4, 2, 4, 4), ("gx_0", "gx_1", "gy_0", "gy_1"))
    in_specs = (
        P(),
        P(),
        P(GX, GY),
        P(GX, GY),
        P(GX, GY),
        P(GX, GY),
        P(GX, GY),
        P(GX, GY),
        P(None, GX, None),
        P(None, None, GY),
        P(None, GY),
        P(None, GX, None),
        P(None, None, GY),
        P(None, GY),
        P(),
        P(),
        P(),
        P(GX_GY, None, None, None),
    )
    out_specs = P(GX, GY)
    return jax.shard_map(local, mesh=split, in_specs=in_specs, out_specs=out_specs, check_vma=False)
```

profile of v0, /device:TPU:1, one launch (start us, length us, event | category | flops | bytes accessed | tf_op | source)
XLA Modules:
  0.0 545.3 jit_solution(1532152101871620547)
XLA Ops:
  6.5 5.4 copy.183
  12.0 32.5 %select_bitcast_fusion.2 = (f32[2048,512,1]{0,1,2:T(8,128)S(1)}, f32[2048,512,1]{0,1,2:T(8,128)S(1)}) fusion(s32[2048,512]{0,1:T(8,128)} %copy.183), kind=kLoop, calls=%fused_computation.196 | loop fusion | flops 210763776 | bytes 12582912 | tf_op jit(solution)/shard_map/stack | solution.py:110
  45.5 11.1 %copy.187 = f32[2048,512,2]{0,2,1:T(2,128)} copy(f32[2048,512,2]{0,1,2:T(8,128)S(1)} %pad_maximum_fusion) | data formatting | bytes 16777216 | tf_op jit(solution)/shard_map/stack | solution.py:110
  56.6 16.0 %stack.34 = f32[32,64,1024]{1,0,2:T(8,128)} reshape(f32[2048,512,2]{0,2,1:T(2,128)} %copy.187) | data formatting | bytes 16777216 | tf_op jit(solution)/shard_map/stack | solution.py:110
  72.7 12.8 %copy.191 = f32[32,64,1024]{2,1,0:T(8,128)} copy(f32[32,64,1024]{1,0,2:T(8,128)} %stack.34) | data formatting | bytes 16777216 | tf_op jit(solution)/shard_map/stack | solution.py:110
  85.5 5.1 multiply_reduce_fusion.1
  90.6 6.8 %all-to-all-start = ((f32[8,1,1,128]{3,2,1,0:T(1,128)}), f32[8,1,1,128]{3,2,1,0:T(1,128)S(1)}, u32[]{:S(2)}, u32[]{:S(2)}) async-start(f32[8,1,1,128]{3,2,1,0:T(1,128)} %bitcast.23), calls=%async_computation | async-start | bytes 8192 | tf_op jit(solution)/shard_map/all_to_all | solution.py:53
  97.4 8.0 %copy.196 = bf16[5,2,256,1024]{2,3,1,0:T(8,128)(2,1)} copy(bf16[5,2,256,1024]{3,2,1,0:T(8,128)(2,1)} %param.39) | data formatting | bytes 10485760 | tf_op jit(solution)/shard_map/while | solution.py:218
  110.2 10.9 %reshape.509 = f32[2048,1024]{0,1:T(8,128)} reshape(f32[2048,512,2]{0,2,1:T(2,128)} %copy.187) | data formatting | bytes 16777216 | tf_op jit(solution)/shard_map/reshape | solution.py:110
  121.4 5.4 copy.203
  126.8 32.5 %select_bitcast_fusion = (f32[2048,512,1]{0,1,2:T(8,128)S(1)}, f32[2048,512]{0,1:T(8,128)S(1)}) fusion(s32[2048,512]{0,1:T(8,128)} %copy.203), kind=kLoop, calls=%fused_computation.191 | loop fusion | flops 210763776 | bytes 12582912 | tf_op jit(solution)/shard_map/stack | solution.py:110
  159.3 3.9 stack.39
  163.2 6.3 %copy.207 = f32[2048,512,1]{0,2,1:T(1,128)} copy(f32[2048,512,1]{0,1,2:T(8,128)S(1)} %get-tuple-element.235) | data formatting | bytes 8388608 | tf_op jit(solution)/shard_map/stack | solution.py:110
  169.7 11.2 %mul.441 = f32[32,64,1024]{1,0,2:T(8,128)} broadcast(f32[32,1024]{0,1:T(8,128)S(1)} %copy.208), dimensions={0,2} | broadcast | bytes 8519680 | tf_op jit(solution)/shard_map/mul | solution.py:113
  180.9 15.8 %mul.442 = f32[2048,512,2]{0,2,1:T(2,128)} reshape(f32[32,64,1024]{1,0,2:T(8,128)} %mul.441) | data formatting | bytes 16777216 | tf_op jit(solution)/shard_map/mul | solution.py:113
  196.8 4.3 mul.398
  201.1 9.3 %copy.188 = f32[2048,1024]{0,1:T(8,128)} copy(f32[2048,1024]{1,0:T(8,128)} %bitcast.238) | data formatting | bytes 16777216 | tf_op jit(solution)/shard_map/mul | solution.py:113
  210.9 9.2 %multiply_convert_fusion.4 = bf16[2048,1024]{0,1:T(8,128)(2,1)} fusion(f32[2048,1024]{0,1:T(8,128)} %reshape.509, f32[2048,1024]{0,1:T(8,128)} %copy.188), kind=kLoop, calls=%fused_computation.60 | loop fusion | flops 4194304 | bytes 20971520 | tf_op jit(solution)/shard_map/convert_element_type | solution.py:113
  220.9 3.4 fusion.145
  225.0 3.9 select_bitcast_fusion.4
  233.3 3.7 fusion.148
  240.0 24.9 %all-reduce = (f32[8,1024]{1,0:T(8,128)S(1)}, f32[8,16,16]{2,1,0:T(8,128)S(1)}, f32[8,128]{1,0:T(8,128)S(1)}, f32[8,16,16]{2,1,0:T(8,128)S(1)}) all-reduce(f32[8,1024]{1,0:T(8,128)S(1)} %fusion.88, f32[8,16,16]{2,1,0:T(8,128)S(1)} %fusion.149, ...), channel_id=1, replica_groups=mesh['gx_0'=4,'gx_1'=2,'gy_0'=4,'gy_1'=4] {'gx_0','gx_1'}, use_global_device_ids=true, to_apply=%region_4.5 | all-reduce | flops 13312 | bytes 106496 | tf_op jit(solution)/shard_map/psum | solution.py:260
  266.0 13.1 %pad_maximum_fusion.1 = (f32[2048,512,2]{0,2,1:T(2,128)}, bf16[2048,512,2]{0,2,1:T(2,128)(2,1)}) fusion(f32[2048,512,1]{0,2,1:T(1,128)} %stack.39, f32[2048,512,1]{0,2,1:T(1,128)} %copy.207, f32[2048,512,2]{0,2,1:T(2,128)} %mul.442), kind=kLoop, calls=%fused_computation.55 | loop fusion | flops 6291456 | bytes 29360128 | tf_op jit(solution)/shard_map/stack | solution.py:110
  284.7 7.1 %all-to-all-start.1 = ((f32[8,8,16,128]{3,2,1,0:T(8,128)}), f32[8,8,16,128]{3,2,1,0:T(8,128)S(1)}, u32[]{:S(2)}, u32[]{:S(2)}) async-start(f32[8,8,16,128]{3,2,1,0:T(8,128)} %bitcast.192), calls=%async_computation.1 | async-start | bytes 1048576 | tf_op jit(solution)/shard_map/all_to_all | solution.py:53
  292.1 16.2 %stack.41 = f32[32,64,1024]{1,0,2:T(8,128)} reshape(f32[2048,512,2]{0,2,1:T(2,128)} %get-tuple-element.231) | data formatting | bytes 16777216 | tf_op jit(solution)/shard_map/stack | solution.py:110
  308.3 18.1 %all_gather.14 = bf16[8,2048]{1,0:T(8,128)(2,1)S(1)} all-gather(bf16[8,128]{1,0:T(8,128)(2,1)S(1)} %fusion.132), channel_id=1, replica_groups=mesh['gx_0'=4,'gx_1'=2,'gy_0'=4,'gy_1'=4] {'gy_0','gy_1'}, dimensions={1}, use_global_device_ids=true | all-gather | bytes 34816 | tf_op jit(solution)/shard_map/all_gather | solution.py:289
  328.1 18.7 %all_gather.12 = f32[8,1024]{1,0:T(8,128)S(1)} all-gather(f32[8,128]{1,0:T(8,128)S(1)} %rsqrt_multiply_fusion.1), channel_id=1, replica_groups=mesh['gx_0'=4,'gx_1'=2,'gy_0'=4,'gy_1'=4] {'gx_0','gx_1'}, dimensions={1}, use_global_device_ids=true | all-gather | bytes 36864 | tf_op jit(solution)/shard_map/all_gather | solution.py:276
  347.2 17.2 %all_gather.13 = bf16[8,16384]{1,0:T(8,128)(2,1)S(1)} all-gather(bf16[8,1024]{1,0:T(8,128)(2,1)S(1)} %maximum_bitcast_fusion), channel_id=1, replica_groups=mesh['gx_0'=4,'gx_1'=2,'gy_0'=4,'gy_1'=4] {'gy_0','gy_1'}, dimensions={1}, use_global_device_ids=true | all-gather | bytes 278528 | tf_op jit(solution)/shard_map/all_gather | solution.py:288
  364.5 12.5 %while.28 = (s32[]{:T(128)}, f32[8,128]{1,0:T(8,128)S(1)}, f32[8,128]{1,0:T(8,128)S(1)}, f32[8,128,128]{2,1,0:T(8,128)S(1)}, s32[]{:T(128)}, /*index=5*/s32[3]{0...) while((s32[]{:T(128)}, f32[8,128]{1,0:T(8,128)S(1)}, ...), condition=%wide.region_13.14_spmd, body=%wide.region_10.13_spmd.sunk | while | flops 59032844 | bytes 3850327 | solution.py:218
  377.3 6.6 %while.29 = (s32[]{:T(128)}, f32[8,128]{1,0:T(8,128)S(1)}, f32[8,128]{1,0:T(8,128)S(1)}, f32[8,128,128]{2,1,0:T(8,128)S(1)}, s32[]{:T(128)}, /*index=5*/s32[2]{0...) while((s32[]{:T(128)}, f32[8,128]{1,0:T(8,128)S(1)}, ...), condition=%wide.region_20.21_spmd, body=%wide.region_17.20_spmd.sunk | while | flops 59032840 | bytes 3850265 | solution.py:218
  383.9 13.3 %pmax.28 = f32[8,128]{1,0:T(8,128)S(1)} all-reduce(f32[8,128]{1,0:T(8,128)S(1)} %max.48), channel_id=1, replica_groups=mesh['gx_0'=4,'gx_1'=2,'gy_0'=4,'gy_1'=4] {'gx_0'}, use_global_device_ids=true, to_apply=%region_22.23 | all-reduce | flops 1024 | bytes 8192 | tf_op jit(solution)/shard_map/pmax | solution.py:64
  397.2 3.4 pmax.29
  400.6 13.1 %pmax.30 = f32[8,128]{1,0:T(8,128)S(1)} all-reduce(f32[8,128]{1,0:T(8,128)S(1)} %pmax.29), channel_id=1, replica_groups=mesh['gx_0'=4,'gx_1'=2,'gy_0'=4,'gy_1'=4] {'gy_0'}, use_global_device_ids=true, to_apply=%region_24.25 | all-reduce | flops 1024 | bytes 8192 | tf_op jit(solution)/shard_map/pmax | solution.py:64
  413.7 7.3 %pmax.31 = f32[8,128]{1,0:T(8,128)S(1)} all-reduce(f32[8,128]{1,0:T(8,128)S(1)} %pmax.30), channel_id=1, replica_groups=mesh['gx_0'=4,'gx_1'=2,'gy_0'=4,'gy_1'=4] {'gy_1'}, use_global_device_ids=true, to_apply=%region_25.26 | all-reduce | flops 1024 | bytes 8192 | tf_op jit(solution)/shard_map/pmax | solution.py:64
  422.5 18.5 %multiply_reduce_fusion = f32[1024]{0:T(1024)} fusion(f32[32,64,1024]{1,0,2:T(8,128)} %stack.41, f32[32,1024]{0,1:T(8,128)S(1)} %copy.208), kind=kLoop, calls=%fused_computation.52 | loop fusion | flops 10484736 | bytes 8523776 | tf_op jit(solution)/shard_map/reduce_sum | solution.py:136
  441.0 7.2 %all-to-all-start.4 = ((f32[8,1,1,128]{3,2,1,0:T(1,128)}), f32[8,1,1,128]{3,2,1,0:T(1,128)S(1)}, u32[]{:S(2)}, u32[]{:S(2)}) async-start(f32[8,1,1,128]{3,2,1,0:T(1,128)} %bitcast.51), calls=%async_computation.5 | async-start | bytes 8192 | tf_op jit(solution)/shard_map/all_to_all | solution.py:53
  448.2 10.9 %reshape.524 = f32[2048,1024]{0,1:T(8,128)} reshape(f32[2048,512,2]{0,2,1:T(2,128)} %get-tuple-element.231) | data formatting | bytes 16777216 | tf_op jit(solution)/shard_map/reshape | solution.py:110
  459.1 4.3 mul.441.clone
  463.4 9.1 %copy.212 = f32[2048,1024]{0,1:T(8,128)} copy(f32[2048,1024]{1,0:T(8,128)} %bitcast.239) | data formatting | bytes 16777216 | tf_op jit(solution)/shard_map/mul | solution.py:113
  472.5 7.3 %fusion.68 = f32[1024,128]{0,1:S(1)} fusion(bf16[2048,128]{0,1:T(8,128)(2,1)S(1)} %bitcast.240, f32[2048,1024]{0,1:T(8,128)} %reshape.524, f32[2048,1024]{0,1:T(8,128)} %copy.212), kind=kOutput, calls=%fused_computation.187 | convolution fusion | flops 541065216 | bytes 17825792
  480.6 4.8 all-to-all-start.5
  487.3 7.6 %all-to-all-done.5 = f32[8,8,16,128]{3,2,1,0:T(8,128)S(1)} async-done(((f32[8,8,16,128]{3,2,1,0:T(8,128)}), f32[8,8,16,128]{3,2,1,0:T(8,128)S(1)}, u32[]{:S(2)}, u32[]{:S(2)}) %all-to-all-start.5) | async-done | bytes 524320 | tf_op jit(solution)/shard_map/all_to_all | solution.py:53
  496.5 3.7 all-to-all-start.2
  500.2 7.3 %convert_element_type.120 = bf16[2048,1024]{0,1:T(8,128)(2,1)} reshape(bf16[2048,512,2]{0,2,1:T(2,128)(2,1)} %get-tuple-element.232) | data formatting | bytes 8388608 | tf_op jit(solution)/shard_map/convert_element_type | solution.py:113
  508.5 13.7 %all_gather.15 = f32[8,1024]{1,0:T(8,128)S(1)} all-gather(f32[8,128]{1,0:T(8,128)S(1)} %rsqrt_multiply_fusion), channel_id=1, replica_groups=mesh['gx_0'=4,'gx_1'=2,'gy_0'=4,'gy_1'=4] {'gx_0','gx_1'}, dimensions={1}, use_global_device_ids=true | all-gather | bytes 36864 | tf_op jit(solution)/shard_map/all_gather | solution.py:277
  524.0 3.4 fusion.116
  528.5 3.4 all-to-all-start.3
  532.1 4.6 all-to-all-done.3
  (167 shorter events, 46.6 us)
Async XLA Ops:
  6.5 204.1 %copy-start = (bf16[8,2048,16]{1,2,0:T(8,128)(2,1)S(1)}, bf16[8,2048,16]{1,2,0:T(8,128)(2,1)}, u32[]{:S(2)}) copy-start(bf16[8,2048,16]{1,2,0:T(8,128)(2,1)} %param.30) | copy-start | bytes 1572868
  72.7 12.8 %copy-start.6 = (f32[32,1024]{1,0:T(8,128)S(1)}, f32[32,1024]{1,0:T(8,128)}, u32[]{:S(2)}) copy-start(f32[32,1024]{1,0:T(8,128)} %param.25) | copy-start | bytes 393220
  90.6 194.1 %all-to-all-start = ((f32[8,1,1,128]{3,2,1,0:T(1,128)}), f32[8,1,1,128]{3,2,1,0:T(1,128)S(1)}, u32[]{:S(2)}, u32[]{:S(2)}) async-start(f32[8,1,1,128]{3,2,1,0:T(1,128)} %bitcast.23), calls=%async_computation | async-start | bytes 8192 | tf_op jit(solution)/shard_map/all_to_all | solution.py:53
  108.4 268.9 %collective-permute-start = (bf16[2,2,256,1024]{2,3,1,0:T(8,128)(2,1)}, bf16[2,2,256,1024]{2,3,1,0:T(8,128)(2,1)}, u32[]{:S(2)}, u32[]{:S(2)}) collective-permute-start(bf16[2,2,256,1024]{2,3,1,0:T(8,128)(2,1)} %slice.75), channel_id=1, source_target_pairs={{0,1},{1,0},{2,3},{3,2},{4,5},{5,4},{6,7},{7,6},{8,9},{9,8},{10,11... | collective-permute-start | bytes 6291464 | tf_op jit(solution)/shard_map/ppermute | solution.py:60
  110.2 10.9 %copy-start.4 = (bf16[8,16384]{1,0:T(8,128)(2,1)S(1)}, bf16[8,16384]{1,0:T(8,128)(2,1)}, u32[]{:S(2)}) copy-start(bf16[8,16384]{1,0:T(8,128)(2,1)} %param.22) | copy-start | bytes 786436
  121.1 103.1 %copy-start.5 = (f32[8,16384]{1,0:T(8,128)}, f32[8,16384]{1,0:T(8,128)S(1)}, u32[]{:S(2)}) copy-start(f32[8,16384]{1,0:T(8,128)S(1)} %convert_element_type.102) | copy-start | bytes 1572868
  163.2 6.3 %copy-start.7 = (f32[32,1024]{1,0:T(8,128)S(1)}, f32[32,1024]{1,0:T(8,128)}, u32[]{:S(2)}) copy-start(f32[32,1024]{1,0:T(8,128)} %param.29) | copy-start | bytes 393220
  180.9 15.8 %copy-start.13 = (s32[8]{0:T(128)S(1)}, s32[8]{0:T(128)}, u32[]{:S(2)}) copy-start(s32[8]{0:T(128)} %param.37) | copy-start | bytes 100
  201.1 9.3 %copy-start.12 = (s32[8]{0:T(128)S(1)}, s32[8]{0:T(128)}, u32[]{:S(2)}) copy-start(s32[8]{0:T(128)} %param.36) | copy-start | bytes 100
  220.1 4.9 copy-start.8
  224.3 7.3 %copy-start.10 = (f32[32,128]{1,0:T(8,128)S(1)}, f32[32,128]{1,0:T(8,128)}, u32[]{:S(2)}) copy-start(f32[32,128]{1,0:T(8,128)} %param.27) | copy-start | bytes 49156
  229.0 4.0 copy-start.2
  233.0 4.1 copy-start.3
  266.0 13.3 %copy-start.11 = (s32[8,96]{1,0:T(8,128)S(1)}, s32[8,96]{1,0:T(8,128)}, u32[]{:S(2)}) copy-start(s32[8,96]{1,0:T(8,128)} %param.38) | copy-start | bytes 9220
  284.7 41.9 %all-to-all-start.1 = ((f32[8,8,16,128]{3,2,1,0:T(8,128)}), f32[8,8,16,128]{3,2,1,0:T(8,128)S(1)}, u32[]{:S(2)}, u32[]{:S(2)}) async-start(f32[8,8,16,128]{3,2,1,0:T(8,128)} %bitcast.192), calls=%async_computation.1 | async-start | bytes 1048576 | tf_op jit(solution)/shard_map/all_to_all | solution.py:53
  291.7 193.7 %reduce-scatter.2.cloned.1.call-start = ((), (), s32[]{:S(2)}) async-start(), calls=%async_computation.7 | async-start | bytes 1179648 | tf_op jit(solution)/shard_map/reduce_scatter | solution.py:70
  441.0 39.6 %all-to-all-start.4 = ((f32[8,1,1,128]{3,2,1,0:T(1,128)}), f32[8,1,1,128]{3,2,1,0:T(1,128)S(1)}, u32[]{:S(2)}, u32[]{:S(2)}) async-start(f32[8,1,1,128]{3,2,1,0:T(1,128)} %bitcast.51), calls=%async_computation.5 | async-start | bytes 8192 | tf_op jit(solution)/shard_map/all_to_all | solution.py:53
  480.6 14.3 %all-to-all-start.5 = ((f32[8,8,16,128]{3,2,1,0:T(8,128)}), f32[8,8,16,128]{3,2,1,0:T(8,128)S(1)}, u32[]{:S(2)}, u32[]{:S(2)}) async-start(f32[8,8,16,128]{3,2,1,0:T(8,128)} %bitcast.190), calls=%async_computation.6 | async-start | bytes 1048576 | tf_op jit(solution)/shard_map/all_to_all | solution.py:53
  496.5 25.8 %all-to-all-start.2 = ((f32[16,1,16512]{2,1,0:T(1,128)}), f32[16,1,16512]{2,1,0:T(1,128)S(1)}, u32[]{:S(2)}, u32[]{:S(2)}) async-start(f32[16,1,16512]{2,1,0:T(1,128)} %broadcast_in_dim.308), calls=%async_computation.3 | async-start | bytes 2113536 | tf_op jit(solution)/shard_map/all_to_all | solution.py:80
  500.2 7.3 %copy-start.9 = (bf16[8,16,1024]{2,1,0:T(8,128)(2,1)S(1)}, bf16[8,16,1024]{2,1,0:T(8,128)(2,1)}, u32[]{:S(2)}) copy-start(bf16[8,16,1024]{2,1,0:T(8,128)(2,1)} %param.34) | copy-start | bytes 786436
  507.5 30.7 %copy-start.1 = (bf16[8,2048,16]{1,2,0:T(8,128)(2,1)S(1)}, bf16[8,2048,16]{1,2,0:T(8,128)(2,1)}, u32[]{:S(2)}) copy-start(bf16[8,2048,16]{1,2,0:T(8,128)(2,1)} %param.30) | copy-start | bytes 1572868
  528.5 8.2 %all-to-all-start.3 = ((f32[8,1,1024]{2,1,0:T(1,128)}), f32[8,1,1024]{2,1,0:T(1,128)S(1)}, u32[]{:S(2)}, u32[]{:S(2)}) async-start(f32[8,1,1024]{2,1,0:T(1,128)} %copy.209), calls=%async_computation.4 | async-start | bytes 65536 | tf_op jit(solution)/shard_map/all_to_all | solution.py:53
Sparse Core Ops, SparseCore 0:
  422.6 28.2 reduce-scatter.1
where the time goes:
time: 555 us; the launch traced here: 545 us
  local copies, waits for them, and re-layouts  191 us (34%)
  blocking collectives  130 us (23%)
  other arithmetic  127 us (23%)
  starting transfers between devices  34.8 us (6%)
  matrix products  27.6 us (5%)
  between operations  17.4 us (3%)
  waiting for transfers between devices  12.2 us (2%)
    another operation x6, other arithmetic, dequantize(): jnp.stack([low_levels, high_levels], axis=-1)  83.2 us
    another operation x7, local copies, waits for them, and re-layouts, dequantize(): jnp.stack([low_levels, high_levels], axis=-1)  67.1 us
    mul x8, local copies, waits for them, and re-layouts, dequantize(): levels * absmax[:, None, :]  55.4 us
    pmax x4, blocking collectives, by_axis(): return functools.reduce(lax.pmax, axes, x)  37.1 us
    all_to_all x5, starting transfers between devices, sum_at_owner(): blocks = lax.all_to_all(cut_along(x, dim, length), axis, 0, 0, tiled=True)  29.4 us
    psum x1, blocking collectives, local(): lax.psum((query_part, keyval_part, q_gram, o_gram), GX)  24.9 us
    reduce_sum x2, other arithmetic, dora_terms(): squares = jnp.sum(weight_float * weight_float, axis=0)[None, None, :]  23.5 us
    reshape x3, local copies, waits for them, and re-layouts, dequantize(): jnp.stack([low_levels, high_levels], axis=-1)  23.5 us
  transfers between devices with their start and end apart: 8, of which 2 were waited for; matrix products, arithmetic and copies ran while one was open for 45% of the time, Pallas kernels for 0%

commit v1 on v0

v1 whole, which is shorter than its diff:
```python
import functools
import math

import jax
import jax.numpy as jnp
import numpy as np
from jax import lax
from jax.experimental import pallas as pl
from jax.experimental.pallas import tpu as pltpu
from jax.sharding import PartitionSpec as P

HEADS = 128
KV_HEADS = 8
HEAD_DIM = 128
TENANTS = 8
RANK = 16
QBLOCK = 64
PAGE = 256
ROWS = 8
NX = 8
NY = 16
SLOTS = 5
LOCAL_IN = 2048
HALF = 512
CHUNK = 256
CHUNKS = LOCAL_IN // CHUNK
D = 16384

NF4_LEVELS = (
    -1.0,
    -0.6961928009986877,
    -0.5250730514526367,
    -0.39491748809814453,
    -0.28444138169288635,
    -0.18477343022823334,
    -0.09105003625154495,
    0.0,
    0.07958029955625534,
    0.16093020141124725,
    0.24611230194568634,
    0.33791524171829224,
    0.44070982933044434,
    0.5626170039176941,
    0.7229568362236023,
    1.0,
)
NORM_EPS = 1e-05
NEG_FILL = -1e30
ROPE_BASE = 500000.0
MESH = pl.DeviceIdType.MESH
F32 = jnp.float32
BF16 = jnp.bfloat16
INV_ROOT = 1.0 / math.sqrt(HEAD_DIM)


def constants():
    table = np.zeros((16, 128), np.float32)
    table[:8, :16] = np.asarray(NF4_LEVELS, np.float32)[None]
    frequency = ROPE_BASE ** (-2.0 * np.arange(64, dtype=np.float64) / HEAD_DIM)
    table[8:] = np.concatenate([frequency, frequency]).astype(np.float32)[None]
    return table


def lookup(table, index):
    numbers = lax.GatherDimensionNumbers(
        offset_dims=(),
        collapsed_slice_dims=(1,),
        start_index_map=(1,),
        operand_batching_dims=(0,),
        start_indices_batching_dims=(0,),
    )
    return lax.gather(
        table,
        index[..., None],
        numbers,
        slice_sizes=(1, 1),
        mode=lax.GatherScatterMode.PROMISE_IN_BOUNDS,
    )


def lanes_of(shape):
    return lax.broadcasted_iota(jnp.int32, shape, 1)


def rows_of(shape):
    return lax.broadcasted_iota(jnp.int32, shape, 0)


def dot(a, b):
    return lax.dot_general(a, b, (((1,), (0,)), ((), ())), preferred_element_type=F32)


def dot_nt(a, b):
    return lax.dot_general(a, b, (((1,), (1,)), ((), ())), preferred_element_type=F32)


def two_parts(x):
    high = x.astype(BF16)
    return high, (x - high.astype(F32)).astype(BF16)


def parted(x):
    n, width = x.shape
    lane = lanes_of((n, 128))
    low = lane < 64
    evens, odds = [], []
    for c in range(width // 256):
        a, b = x[:, 256 * c : 256 * c + 128], x[:, 256 * c + 128 : 256 * c + 256]
        at = (2 * lane) & 127
        evens.append(jnp.where(low, lookup(a, at), lookup(b, at)))
        odds.append(jnp.where(low, lookup(a, at + 1), lookup(b, at + 1)))
    return jnp.concatenate(evens, axis=1), jnp.concatenate(odds, axis=1)


def joined(even, odd):
    n, width = even.shape
    lane = lanes_of((n, 128))
    is_even = (lane & 1) == 0
    blocks = []
    for c in range(width // 64):
        part = slice(128 * (c // 2), 128 * (c // 2) + 128)
        at = 64 * (c % 2) + (lane >> 1)
        blocks.append(jnp.where(is_even, lookup(even[:, part], at), lookup(odd[:, part], at)))
    return blocks


def kernel(
    tenant,
    lengths,
    hidden,
    gain,
    q_codes,
    q_absmax,
    kv_codes,
    kv_absmax,
    o_codes,
    o_absmax,
    q_down,
    q_up,
    q_magnitude,
    o_down,
    o_up,
    o_magnitude,
    pages,
    cache,
    consts,
    out,
    hid_v,
    gain_v,
    qc_v,
    qa_v,
    kc_v,
    ka_v,
    oc_v,
    oa_v,
    qd_v,
    qu_v,
    qm_v,
    od_v,
    ou_v,
    om_v,
    pt_v,
    cache_v,
    const_v,
    ae_v,
    ao_v,
    up_v,
    lhs_v,
    we_v,
    wo_v,
    acc_v,
    sq_v,
    flat_v,
    kvw_v,
    qf_v,
    score_v,
    num_v,
    nbf_v,
    att_v,
    b_src,
    b_dst,
    c1_src,
    c1_dst,
    c2_src,
    c2_dst,
    n_src,
    n_dst,
    s_src,
    s_dst,
    e2_src,
    e2_dst,
    e3_src,
    e3_dst,
    g_src,
    g_dst,
    load_sem,
    code_sem,
    page_sem,
    bs,
    br,
    c1s,
    c1r,
    c2s,
    c2r,
    ns,
    nr,
    ss,
    sr,
    e2s,
    e2r,
    e3s,
    e3r,
    gs,
    gr,
):
    gx = lax.axis_index("gx")
    gy = lax.axis_index("gy")

    def load(n, src, dst):
        copy = pltpu.make_async_copy(src, dst, load_sem.at[n])
        copy.start()
        return copy

    in_at = pl.multiple_of(gx * LOCAL_IN, LOCAL_IN)
    head_at = pl.multiple_of(gx * HEAD_DIM, HEAD_DIM)
    loads = [
        load(0, hidden, hid_v),
        load(1, gain.at[pl.ds(pl.multiple_of(gx * 16, 16), 16), :], gain_v),
        load(2, consts, const_v),
        load(3, q_absmax, qa_v),
        load(4, q_down, qd_v),
        load(5, q_up, qu_v),
    ]
    q_loads = []
    for c in range(CHUNKS):
        part = pl.ds(c * CHUNK, CHUNK)
        q_loads.append(pltpu.make_async_copy(q_codes.at[part, :], qc_v.at[part, :], code_sem.at[c]))
        q_loads[-1].start()
    later = [
        load(6, kv_codes, kc_v),
        load(7, kv_absmax, ka_v),
        load(8, q_magnitude.at[:, pl.ds(head_at, HEAD_DIM)], qm_v),
        load(9, pages, pt_v),
    ]
    o_small = [load(10, o_absmax, oa_v), load(11, o_down, od_v), load(12, o_up, ou_v), load(13, o_magnitude, om_v)]
    o_loads = []
    for c in range(CHUNKS):
        part = pl.ds(c * CHUNK, CHUNK)
        o_loads.append(
            pltpu.make_async_copy(o_codes.at[part, :], oc_v.at[part, :], code_sem.at[CHUNKS + c])
        )
        o_loads[-1].start()
    page_loads = []
    for s in range(SLOTS):
        page_loads.append(pltpu.make_async_copy(cache.at[s], cache_v.at[s], page_sem.at[s]))
        page_loads[-1].start()

    barrier = pltpu.get_barrier_semaphore()
    for k in range(1, NX):
        pl.semaphore_signal(
            barrier, inc=1, device_id={"gx": lax.rem(gx + k, NX)}, device_id_type=MESH
        )
    for k in range(1, NY):
        pl.semaphore_signal(
            barrier, inc=1, device_id={"gy": lax.rem(gy + k, NY)}, device_id_type=MESH
        )

    def to_gx(k, src, dst, send, recv):
        return pltpu.make_async_remote_copy(
            src_ref=src,
            dst_ref=dst,
            send_sem=send.at[k],
            recv_sem=recv.at[k],
            device_id={"gx": lax.rem(gx + k, NX)},
            device_id_type=MESH,
        )

    def to_gy(k, src, dst, send, recv):
        return pltpu.make_async_remote_copy(
            src_ref=src,
            dst_ref=dst,
            send_sem=send.at[k],
            recv_sem=recv.at[k],
            device_id={"gy": lax.rem(gy + k, NY)},
            device_id_type=MESH,
        )

    started = []

    for copy in loads:
        copy.wait()

    row8 = rows_of((ROWS, 128))
    lane8 = lanes_of((ROWS, 128))
    tenant_of = jnp.zeros((ROWS, 128), jnp.int32)
    length_of = jnp.zeros((ROWS, 128), jnp.int32)
    for r in range(ROWS):
        tenant_of = jnp.where(row8 == r, tenant[r], tenant_of)
        length_of = jnp.where(row8 == r, lengths[r], length_of)
    angles = length_of.astype(F32) * const_v[8:16, :]
    cosine = jnp.cos(angles)
    sine = jnp.sin(angles)
    sine = jnp.where(lane8 < 64, -sine, sine)

    def rope(x):
        return x * cosine + pltpu.roll(x, 64, 1) * sine

    total = jnp.zeros((ROWS, 128), F32)
    for c in range(D // 1024):
        x = hid_v[:, c * 1024 : (c + 1) * 1024].astype(F32)
        x = x * x
        for j in range(8):
            total = total + x[:, j * 128 : (j + 1) * 128]
    inverse = lax.rsqrt(jnp.sum(total, axis=1, keepdims=True) * (1.0 / D) + NORM_EPS)
    states = hid_v[:, pl.ds(in_at, LOCAL_IN)].astype(F32)
    lhs_v[0:16, :] = jnp.zeros((16, LOCAL_IN), BF16)
    normed = []
    for c in range(16):
        x = states[:, c * 128 : (c + 1) * 128] * inverse * gain_v[c : c + 1, :]
        normed.append(x)
    normed = jnp.concatenate(normed, axis=1)
    lhs_v[0:16, :] = jnp.concatenate([normed, jnp.zeros_like(normed)], axis=0).astype(BF16)
    lhs_v[16:144, :] = qd_v[...]

    lane64 = lanes_of((64, 128))
    table = jnp.broadcast_to(const_v[0:1, :], (64, 128))

    def dequantize(codes, row, scale_row):
        for c in range(4):
            cols = slice(128 * c, 128 * c + 128)
            words = codes[pl.ds(row, 64), cols]
            for half, (scales, ref) in enumerate(((ae_v, we_v), (ao_v, wo_v))):
                code = words & 15 if half == 0 else words >> 4
                value = lookup(table, code) * scales[c, pl.ds(scale_row, 1), :]
                ref[pl.ds(row, 64), cols] = value.astype(BF16)
                square = value * value
                part = square[0:8]
                for j in range(1, 8):
                    part = part + square[8 * j : 8 * j + 8]
                sq_v[half, :, cols] += part

    def weight_chunks(codes, first, last, lhs_rows):
        def chunk(c, carry):
            base = pl.multiple_of(c * CHUNK, CHUNK)
            for b in range(CHUNK // QBLOCK):
                row = pl.multiple_of(c * CHUNK + b * QBLOCK, QBLOCK)
                dequantize(codes, row, c * (CHUNK // QBLOCK) + b)
            left = lhs_v[lhs_rows, pl.ds(base, CHUNK)]
            acc_v[0, lhs_rows, :] += dot(left, we_v[pl.ds(base, CHUNK), :])
            acc_v[1, lhs_rows, :] += dot(left, wo_v[pl.ds(base, CHUNK), :])
            return carry

        lax.fori_loop(first, last, chunk, 0)

    def begin_projection(absmax, up):
        even, odd = parted(absmax[...])
        for c in range(4):
            ae_v[c] = even[:, 128 * c : 128 * c + 128]
            ao_v[c] = odd[:, 128 * c : 128 * c + 128]
        for c in range(4):
            even, odd = parted(up[:, 256 * c : 256 * c + 256].astype(F32))
            up_v[0, :, 128 * c : 128 * c + 128] = even.astype(BF16)
            up_v[1, :, 128 * c : 128 * c + 128] = odd.astype(BF16)
        acc_v[...] = jnp.zeros_like(acc_v)
        sq_v[...] = jnp.zeros_like(sq_v)

    def norm_parts(gram):
        same = (rows_of((128, 128)) >> 4) == (lanes_of((128, 128)) >> 4)
        high, low = two_parts(jnp.where(same, gram, 0.0))
        halves = []
        for half in range(2):
            up = up_v[half]
            inner = 2.0 * acc_v[half, 16:144, :] + (dot(high, up) + dot(low, up))
            terms = jnp.sum((up.astype(F32) * inner).reshape(TENANTS, RANK, HALF), axis=1)
            terms = terms + jnp.sum(sq_v[half], axis=0, keepdims=True)
            mine = tenant_of[:, 0:1]
            chosen = jnp.zeros((ROWS, HALF), F32)
            for t in range(TENANTS):
                chosen = jnp.where(mine == t, terms[t : t + 1, :], chosen)
            halves.append(chosen)
        return halves

    def adapter(middle):
        masked = jnp.where(tenant_of == (lane8 >> 4), middle, 0.0)
        high = masked.astype(BF16).astype(F32)
        both = jnp.concatenate([high, masked - high], axis=0).astype(BF16)
        halves = []
        for half in range(2):
            x = dot(both, up_v[half])
            halves.append(x[0:8] + x[8:16])
        return halves

    begin_projection(qa_v, qu_v)
    for copy in later:
        copy.wait()

    lane32 = lanes_of((32, 128))
    at = jnp.where(lane32 < 64, 2 * lane32, 2 * lane32 - 127)
    kv_scale = jnp.concatenate(
        [lookup(ka_v[...], at), jnp.zeros((96, 128), F32)], axis=0
    ).T
    for c in range(16):
        words = kc_v[:, c * 128 : (c + 1) * 128]
        for half in range(2):
            code = words & 15 if half == 0 else words >> 4
            scale = lookup(kv_scale[64 * half : 64 * half + 64], 2 * c + (lane64 >> 6))
            kvw_v[64 * half : 64 * half + 64, c * 128 : (c + 1) * 128] = (
                lookup(table, code) * scale
            ).astype(BF16)
    keyval = dot_nt(lhs_v[0:16, :], kvw_v[...])[0:8]
    keyval = lookup(keyval, jnp.where((lane8 & 1) == 0, lane8 >> 1, 64 + (lane8 >> 1)))

    inner = dot_nt(lhs_v[...], lhs_v[16:144, :])
    middle, gram = inner[0:8], inner[16:144]

    for copy in q_loads:
        copy.wait()
    weight_chunks(qc_v, 0, CHUNKS, slice(0, 144))

    extra = adapter(middle)
    product = joined(acc_v[0, 0:8, :] + extra[0], acc_v[1, 0:8, :] + extra[1])
    norms = joined(*norm_parts(gram))
    for i in range(NX):
        b_src[i, 0] = product[i]
        b_src[i, 1] = norms[i]
        b_src[i, 2] = keyval

    pl.semaphore_wait(barrier, NX - 1 + NY - 1)

    b_copies = []
    for k in range(1, NX):
        peer = lax.rem(gx + k, NX)
        b_copies.append(to_gx(k, b_src.at[peer], b_dst.at[k], bs, br))
        b_copies[-1].start()
    started += b_copies

    for copy in o_small:
        copy.wait()
    for copy in o_loads:
        copy.wait()
    begin_projection(oa_v, ou_v)
    lhs_v[16:144, :] = od_v[...]
    o_gram = dot_nt(lhs_v[16:144, :], lhs_v[16:144, :])
    down_rows = slice(16, 144)
    weight_chunks(oc_v, 0, 2, down_rows)

    summed = [b_src[gx, j] for j in range(3)]
    for copy in b_copies:
        copy.wait_recv()
    for k in range(1, NX):
        for j in range(3):
            summed[j] = summed[j] + b_dst[k, j]
    magnitude = jnp.zeros((ROWS, 128), F32)
    for t in range(TENANTS):
        magnitude = jnp.where(tenant_of == t, qm_v[t : t + 1, :], magnitude)
    query = rope(summed[0] * (magnitude * lax.rsqrt(summed[1])))
    new = jnp.where(gy < KV_HEADS, rope(summed[2]), summed[2])
    c1_src[...] = jnp.concatenate([query, new], axis=0).astype(BF16)
    c1_dst[gy] = c1_src[...]
    c1_copies = []
    for k in range(1, NY):
        c1_copies.append(to_gy(k, c1_src, c1_dst.at[gy], c1s, c1r))
        c1_copies[-1].start()
    started += c1_copies
    weight_chunks(oc_v, 2, 4, down_rows)

    for copy in c1_copies:
        copy.wait_recv()
    for j in range(NY // 2):
        pair = [c1_dst[2 * j + n].astype(F32)[0:8] for n in range(2)]
        c2_src[16 * j : 16 * j + 16, :] = jnp.concatenate(pair, axis=0).astype(BF16)
    c2_dst[gx] = c2_src[...]
    c2_copies = []
    for k in range(1, NX):
        c2_copies.append(to_gx(k, c2_src, c2_dst.at[gx], c2s, c2r))
        c2_copies[-1].start()
    started += c2_copies
    weight_chunks(oc_v, 4, CHUNKS, down_rows)
    o_norms = joined(*norm_parts(o_gram))
    for i in range(8):
        flat_v[8 * i : 8 * i + 8, :] = o_norms[i]
    for r in range(ROWS):
        g_src[r, 1] = flat_v[pl.ds(r, 8, stride=8), :]

    page_no = lanes_of((ROWS, 96))
    row_no = rows_of((ROWS, 96))
    length = length_of[:, 0:96]
    live = page_no * PAGE < length
    remaining = jnp.clip(length - page_no * PAGE, 0, PAGE)
    table_pages = pt_v[...]

    def whole(x):
        return jnp.sum(jnp.sum(x.astype(F32), axis=1, keepdims=True), axis=0, keepdims=True)

    owner, filled = [], []
    for s in range(SLOTS):
        hit = jnp.logical_and(table_pages == (gx * NY + gy) * SLOTS + s, live)
        owner.append(whole(jnp.where(hit, row_no, 0)))
        filled.append(whole(jnp.where(hit, remaining, 0)))

    def same(a, b):
        return jnp.where(a == b, 1.0, 0.0).astype(F32)

    for copy in c2_copies:
        copy.wait_recv()
    for i in range(NX):
        block = c2_dst[i].astype(F32)
        for j in range(NY):
            qf_v[pl.ds(8 * j + i, 8, stride=HEADS), :] = block[8 * j : 8 * j + 8]

    even_group = ((rows_of((HEADS, 128)) >> 4) & 1) == 0
    token = lanes_of((HEADS, PAGE)).astype(F32)
    peaks = []
    for s in range(SLOTS):
        q = jnp.zeros((HEADS, HEAD_DIM), F32)
        for r in range(ROWS):
            q = q + qf_v[r * HEADS : (r + 1) * HEADS, :] * same(owner[s], float(r))
        q = jnp.concatenate(
            [jnp.where(even_group, q, 0.0), jnp.where(even_group, 0.0, q)], axis=1
        ).astype(BF16)
        page_loads[s].wait()
        parts = [
            dot_nt(q[32 * p : 32 * p + 32], cache_v[s, 0, :, 256 * p : 256 * p + 256])
            for p in range(4)
        ]
        score = jnp.concatenate(parts, axis=0) * INV_ROOT
        score = jnp.where(token < filled[s], score, NEG_FILL)
        score_v[s] = score
        peaks.append(jnp.max(score, axis=1, keepdims=True))
    totals = []
    for s in range(SLOTS):
        peak = peaks[s]
        for other in range(SLOTS):
            if other != s:
                alike = owner[s] == owner[other]
                peak = jnp.maximum(peak, jnp.where(alike, peaks[other], NEG_FILL))
        weights = jnp.where(token < filled[s], jnp.exp(score_v[s] - peak), 0.0).astype(BF16)
        totals.append(jnp.sum(weights.astype(F32), axis=1, keepdims=True))
        for p in range(4):
            x = dot(weights[32 * p : 32 * p + 32], cache_v[s, 1, :, 256 * p : 256 * p + 256])
            num_v[s, 32 * p : 32 * p + 16, :] = x[0:16, 0:128]
            num_v[s, 32 * p + 16 : 32 * p + 32, :] = x[16:32, 128:256]
    lane_h = lanes_of((HEADS, 128))
    stats = jnp.zeros((HEADS, 128), F32)
    for r in range(ROWS):
        number = jnp.zeros((HEADS, HEAD_DIM), F32)
        peak = jnp.full((HEADS, 1), NEG_FILL, F32)
        total = jnp.zeros((HEADS, 1), F32)
        for s in range(SLOTS):
            mine = same(owner[s], float(r))
            number = number + num_v[s] * mine
            total = total + totals[s] * mine
            peak = jnp.maximum(peak, jnp.where(owner[s] == float(r), peaks[s], NEG_FILL))
        nbf_v[pl.ds(r, HEADS, stride=ROWS), :] = number
        stats = jnp.where(lane_h == r, peak, stats)
        stats = jnp.where(lane_h == 8 + r, total, stats)
    s_src[...] = stats.T[0:16]
    n_src[...] = nbf_v[...].astype(BF16)

    n_copies = []
    for k in range(1, NX):
        peer = lax.rem(gx + k, NX)
        part = pl.ds(pl.multiple_of(peer * 128, 128), 128)
        n_copies.append(to_gx(k, s_src, s_dst.at[k], ss, sr))
        n_copies[-1].start()
        n_copies.append(to_gx(k, n_src.at[part, :], n_dst.at[k], ns, nr))
        n_copies[-1].start()
    started += n_copies

    own_q = qf_v[pl.ds(16 * gx + gy, 8, stride=HEADS), :]
    new_key = c1_dst[gx].astype(F32)[8:16]
    new_value = c1_dst[KV_HEADS + gx].astype(F32)[8:16]
    self_score = jnp.sum(own_q * new_key, axis=1, keepdims=True) * INV_ROOT

    for copy in n_copies:
        copy.wait_recv()
    n_dst[0] = n_src[pl.ds(pl.multiple_of(gx * 128, 128), 128), :]
    s_dst[0] = s_src[...]
    peak = s_dst[0, 0:8]
    for k in range(1, NX):
        peak = jnp.maximum(peak, s_dst[k, 0:8])
    total = jnp.zeros((ROWS, 128), F32)
    shift = lax.rem(128 - 16 * gx, 128)
    factors = []
    for k in range(NX):
        factor = jnp.exp(s_dst[k, 0:8] - peak)
        total = total + factor * s_dst[k, 8:16]
        factors.append(pltpu.roll(factor, shift, 1))
    peak = pltpu.roll(peak, shift, 1)
    total = pltpu.roll(total, shift, 1)
    for j in range(NY // 2):
        pair = [jnp.zeros((ROWS, 128), F32), jnp.zeros((ROWS, 128), F32)]
        for k in range(NX):
            block = n_dst[k, 16 * j : 16 * j + 16, :].astype(F32)
            for n in range(2):
                h = 2 * j + n
                pair[n] = pair[n] + block[8 * n : 8 * n + 8] * factors[k][:, h : h + 1]
        for n in range(2):
            h = 2 * j + n
            e2_src[h, 0] = pair[n]
            e2_src[h, 1] = jnp.where(lane8 < 64, peak[:, h : h + 1], total[:, h : h + 1])

    e2_copies = []
    for k in range(1, NY):
        peer = lax.rem(gy + k, NY)
        e2_copies.append(to_gy(k, e2_src.at[peer], e2_dst.at[k], e2s, e2r))
        e2_copies[-1].start()
    started += e2_copies
    for copy in e2_copies:
        copy.wait_recv()
    e2_dst[0] = e2_src[gy]
    peak = self_score
    for k in range(NY):
        peak = jnp.maximum(peak, e2_dst[k, 1][:, 0:1])
    own = jnp.exp(self_score - peak)
    number = own * new_value
    total = own
    for k in range(NY):
        both = e2_dst[k, 1]
        factor = jnp.exp(both[:, 0:1] - peak)
        number = number + factor * e2_dst[k, 0]
        total = total + factor * both[:, 64:65]
    e3_src[...] = (number / total).astype(BF16).astype(F32)
    e3_dst[gy] = e3_src[...]
    e3_copies = []
    for k in range(1, NY):
        e3_copies.append(to_gy(k, e3_src, e3_dst.at[gy], e3s, e3r))
        e3_copies[-1].start()
    started += e3_copies
    for copy in e3_copies:
        copy.wait_recv()

    for j in range(NY):
        x = e3_dst[j]
        att_v[:, 128 * j : 128 * j + 128] = jnp.concatenate([x, jnp.zeros_like(x)], axis=0).astype(BF16)
    attended = att_v[...]
    middle = dot_nt(attended, lhs_v[16:144, :])[0:8]
    extra = adapter(middle)
    projected = joined(
        dot(attended, we_v[...])[0:8] + extra[0], dot(attended, wo_v[...])[0:8] + extra[1]
    )
    for i in range(8):
        flat_v[8 * i : 8 * i + 8, :] = projected[i]
    for r in range(ROWS):
        g_src[r, 0] = flat_v[pl.ds(r, 8, stride=8), :]
    g_copies = []
    for k in range(1, NX):
        peer = lax.rem(gx + k, NX)
        g_copies.append(to_gx(k, g_src.at[peer], g_dst.at[k], gs, gr))
        g_copies[-1].start()
    started += g_copies

    states = hid_v[:, pl.ds(pl.multiple_of(gy * 1024, 1024), 1024)].astype(F32)
    mine = tenant[gx]
    magnitude = jnp.zeros((8, 128), F32)
    for i in range(8):
        flat_v[8 * i : 8 * i + 8, :] = om_v[:, 128 * i : 128 * i + 128]
    for t in range(TENANTS):
        magnitude = jnp.where(mine == t, flat_v[pl.ds(t, 8, stride=8), :], magnitude)
    for i in range(8):
        flat_v[8 * i : 8 * i + 8, :] = states[:, 128 * i : 128 * i + 128]
    residual = flat_v[pl.ds(gx, 8, stride=8), :]
    summed = [g_src[gx, j] for j in range(2)]
    for copy in g_copies:
        copy.wait_recv()
    for k in range(1, NX):
        for j in range(2):
            summed[j] = summed[j] + g_dst[k, j]
    out[...] = residual + summed[0] * (magnitude * lax.rsqrt(summed[1]))
    for copy in started:
        copy.wait_send()


def local(
    hidden,
    norm_gain,
    q_codes,
    q_absmax,
    kv_codes,
    kv_absmax,
    o_codes,
    o_absmax,
    q_down,
    q_up,
    q_magnitude,
    o_down,
    o_up,
    o_magnitude,
    tenant,
    lengths,
    page_table,
    kv_cache,
):
    def down_rows(down):
        return jnp.transpose(down, (0, 2, 1)).reshape(TENANTS * RANK, LOCAL_IN)

    def up_rows(up):
        return up.reshape(TENANTS * RANK, 1024)

    vmem = pltpu.VMEM
    dma = pltpu.SemaphoreType.DMA
    hbm = pl.BlockSpec(memory_space=pl.ANY)
    smem = pl.BlockSpec(memory_space=pltpu.SMEM)
    scratch = [
        vmem((8, D), BF16),
        vmem((16, 128), F32),
        vmem((LOCAL_IN, HALF), jnp.int32),
        vmem((32, 1024), F32),
        vmem((64, LOCAL_IN), jnp.int32),
        vmem((32, 128), F32),
        vmem((LOCAL_IN, HALF), jnp.int32),
        vmem((32, 1024), F32),
        vmem((128, LOCAL_IN), BF16),
        vmem((128, 1024), BF16),
        vmem((8, 128), F32),
        vmem((128, LOCAL_IN), BF16),
        vmem((128, 1024), BF16),
        vmem((8, 1024), F32),
        vmem((8, 96), jnp.int32),
        vmem((SLOTS, 2, PAGE, 1024), BF16),
        vmem((16, 128), F32),
        vmem((4, 32, 128), F32),
        vmem((4, 32, 128), F32),
        vmem((2, 128, HALF), BF16),
        vmem((144, LOCAL_IN), BF16),
        vmem((LOCAL_IN, HALF), BF16),
        vmem((LOCAL_IN, HALF), BF16),
        vmem((2, 144, HALF), F32),
        vmem((2, 8, HALF), F32),
        vmem((64, 128), F32),
        vmem((128, LOCAL_IN), BF16),
        vmem((ROWS * HEADS, HEAD_DIM), F32),
        vmem((SLOTS, HEADS, PAGE), F32),
        vmem((SLOTS, HEADS, HEAD_DIM), F32),
        vmem((ROWS * HEADS, HEAD_DIM), F32),
        vmem((16, LOCAL_IN), BF16),
        vmem((NX, 3, 8, 128), F32),
        vmem((NX, 3, 8, 128), F32),
        vmem((16, 128), BF16),
        vmem((NY, 16, 128), BF16),
        vmem((128, 128), BF16),
        vmem((NX, 128, 128), BF16),
        vmem((ROWS * HEADS, HEAD_DIM), BF16),
        vmem((NX, 128, 128), BF16),
        vmem((16, 128), F32),
        vmem((NX, 16, 128), F32),
        vmem((NY, 2, 8, 128), F32),
        vmem((NY, 2, 8, 128), F32),
        vmem((8, 128), F32),
        vmem((NY, 8, 128), F32),
        vmem((NX, 2, 8, 128), F32),
        vmem((NX, 2, 8, 128), F32),
        dma((14,)),
        dma((2 * CHUNKS,)),
        dma((SLOTS,)),
        dma((NX,)),
        dma((NX,)),
        dma((NY,)),
        dma((NY,)),
        dma((NX,)),
        dma((NX,)),
        dma((NX,)),
        dma((NX,)),
        dma((NX,)),
        dma((NX,)),
        dma((NY,)),
        dma((NY,)),
        dma((NY,)),
        dma((NY,)),
        dma((NX,)),
        dma((NX,)),
    ]
    result = pl.pallas_call(
        kernel,
        out_shape=jax.ShapeDtypeStruct((8, 128), F32),
        in_specs=[smem, smem] + [hbm] * 17,
        out_specs=pl.BlockSpec(memory_space=pltpu.VMEM),
        scratch_shapes=scratch,
        compiler_params=pltpu.CompilerParams(
            collective_id=0, has_side_effects=True, vmem_limit_bytes=56 * 1024 * 1024
        ),
        name="layer",
    )(
        tenant,
        lengths,
        hidden,
        norm_gain.reshape(128, 128),
        q_codes,
        q_absmax,
        kv_codes.T,
        kv_absmax,
        o_codes,
        o_absmax,
        down_rows(q_down),
        up_rows(q_up),
        q_magnitude,
        down_rows(o_down),
        up_rows(o_up),
        o_magnitude,
        page_table,
        kv_cache,
        jnp.asarray(constants()),
    )
    return result.reshape(1, 1024).astype(BF16)


def solution(mesh):
    in_specs = (
        P(),
        P(),
        P("gx", "gy"),
        P("gx", "gy"),
        P("gx", "gy"),
        P("gx", "gy"),
        P("gx", "gy"),
        P("gx", "gy"),
        P(None, "gx", None),
        P(None, None, "gy"),
        P(None, "gy"),
        P(None, "gx", None),
        P(None, None, "gy"),
        P(None, "gy"),
        P(),
        P(),
        P(),
        P(("gx", "gy"), None, None, None),
    )
    return jax.shard_map(
        local, mesh=mesh, in_specs=in_specs, out_specs=P("gx", "gy"), check_vma=False
    )
```

time: 555 us -> 61.2 us (0.11); the launches traced: 545 us -> 61.1 us
  local copies, waits for them, and re-layouts: 191 us -> 0.6 us
  blocking collectives: 130 us -> 0 us
  other arithmetic: 127 us -> 0.69 us
  Pallas kernels: 0 us -> 59.8 us
  starting transfers between devices: 34.8 us -> 0 us
  matrix products: 27.6 us -> 0 us
  between operations: 17.4 us -> 0.01 us
  waiting for transfers between devices: 12.2 us -> 0 us
    another operation x7 -> x0, other arithmetic: 83.2 us -> none  [the longest x6 83.2 us: dequantize(): jnp.stack([low_levels, high_levels], axis=-1)]
    all_gather x4 -> x0, blocking collectives: 67.7 us -> none  [the longest x1 18.7 us: local(): lax.all_gather(q_scale_share, GX, axis=1, tiled=True)]
    another operation x8 -> x0, local copies, waits for them, and re-layouts: 67.2 us -> none  [the longest x7 67.1 us: dequantize(): jnp.stack([low_levels, high_levels], axis=-1)]
    pallas_call x0 -> x1, Pallas kernels: none -> 59.8 us  [local(): pl.pallas_call(kernel, out_shape=jax.ShapeDtypeStruct((8, 128), F32), in_...]
    mul x9 -> x0, local copies, waits for them, and re-layouts: 55.5 us -> none  [the longest x8 55.4 us: dequantize(): levels * absmax[:, None, :]]
    pmax x4 -> x0, blocking collectives: 37.1 us -> none  [by_axis(): return functools.reduce(lax.pmax, axes, x)]
    all_to_all x6 -> x0, starting transfers between devices: 33.1 us -> none  [the longest x5 29.4 us: sum_at_owner(): blocks = lax.all_to_all(cut_along(x, dim, length), axis, 0, 0, tiled=True)]
    reduce_sum x15 -> x0, other arithmetic: 27.1 us -> none  [the longest x2 23.5 us: dora_terms(): squares = jnp.sum(weight_float * weight_float, axis=0)[None, None, :]]
  transfers between devices with their start and end apart: 8 -> 0, of which waited for: 2 -> 0; matrix products, arithmetic and copies ran while one was open for 45% -> 0% of each run, Pallas kernels for 0% -> 0%
where the time goes in v1:
time: 61.2 us; the launch traced here: 61.1 us
  Pallas kernels  59.8 us (98%)
  other arithmetic  0.69 us (1%)
    pallas_call x1, Pallas kernels, local(): pl.pallas_call(kernel, out_shape=jax.ShapeDtypeStruct((8, 128), F32), in_...  59.8 us

profile of v1, /device:TPU:1, one launch (start us, length us, event | category | flops | bytes accessed | tf_op | source)
XLA Modules:
  0.0 61.1 jit_solution(8606375053583601789)
XLA Ops:
  0.0 59.8 %layer.1 = f32[8,128]{1,0:T(8,128)} custom-call(s32[8]{0:T(128)} %tenant.1, s32[8]{0:T(128)} %lengths.1, bf16[8,16384]{1,0:T(8,128)(2,1)} %hidden.1, f32[128,128]{1,0:T(8,128)} %bitcast.21, s32[2048,512]{1,0:T(8,128)} %q_codes.1, f32[32,1024]{1,0:T(8,128)} %q_absmax.1, s32[64,2048]{1,0:T(8,128)} %bitcast.16, f32[32,128]{1,0:T(8,128)} %kv_absmax.1, ...), custom_call_target="tpu_custom_call" | custom-call | tf_op jit(solution)/shard_map/layer/pallas_call | solution.py:773
  59.8 0.7 %convert_bitcast_fusion = bf16[1,1,8,128]{3,2,1,0:T(8,128)(2,1)S(1)} fusion(f32[8,128]{1,0:T(8,128)} %layer.1), kind=kLoop, calls=%fused_computation.1 | loop fusion | flops 1024 | bytes 6144
  60.5 0.6 copy.22

commit v2 on v1

--- a/solution.py
+++ b/solution.py
@@ -54,10 +54,10 @@
 
 
 def constants():
-    table = np.zeros((16, 128), np.float32)
-    table[:8, :16] = np.asarray(NF4_LEVELS, np.float32)[None]
+    table = np.zeros((24, 128), np.float32)
+    table[:16] = np.asarray(NF4_LEVELS, np.float32)[:, None]
     frequency = ROPE_BASE ** (-2.0 * np.arange(64, dtype=np.float64) / HEAD_DIM)
-    table[8:] = np.concatenate([frequency, frequency]).astype(np.float32)[None]
+    table[16:] = np.concatenate([frequency, frequency]).astype(np.float32)[None]
     return table
 
 
@@ -78,6 +78,32 @@
     )
 
 
+def levels(tables, code):
+    numbers = lax.GatherDimensionNumbers(
+        offset_dims=(),
+        collapsed_slice_dims=(0,),
+        start_index_map=(0,),
+        operand_batching_dims=(1,),
+        start_indices_batching_dims=(1,),
+    )
+
+    def pick(table, index):
+        return lax.gather(
+            table,
+            index[..., None],
+            numbers,
+            slice_sizes=(1, 1),
+            mode=lax.GatherScatterMode.PROMISE_IN_BOUNDS,
+        )
+
+    parts = []
+    for j in range(code.shape[0] // 8):
+        part = code[8 * j : 8 * j + 8]
+        at = part & 7
+        parts.append(jnp.where((part & 8) != 0, pick(tables[1], at), pick(tables[0], at)))
+    return jnp.concatenate(parts, axis=0)
+
+
 def lanes_of(shape):
     return lax.broadcasted_iota(jnp.int32, shape, 1)
 
@@ -99,17 +125,16 @@
     return high, (x - high.astype(F32)).astype(BF16)
 
 
-def parted(x):
-    n, width = x.shape
-    lane = lanes_of((n, 128))
-    low = lane < 64
-    evens, odds = [], []
-    for c in range(width // 256):
-        a, b = x[:, 256 * c : 256 * c + 128], x[:, 256 * c + 128 : 256 * c + 256]
-        at = (2 * lane) & 127
-        evens.append(jnp.where(low, lookup(a, at), lookup(b, at)))
-        odds.append(jnp.where(low, lookup(a, at + 1), lookup(b, at + 1)))
-    return jnp.concatenate(evens, axis=1), jnp.concatenate(odds, axis=1)
+def three_parts(x):
+    high = x.astype(BF16)
+    rest = x - high.astype(F32)
+    middle = rest.astype(BF16)
+    return [high, middle, (rest - middle.astype(F32)).astype(BF16)]
+
+
+def even_first():
+    row, lane = rows_of((256, 256)), lanes_of((256, 256))
+    return jnp.where(row == jnp.where(lane < 128, 2 * lane, 2 * lane - 255), 1.0, 0.0).astype(BF16)
 
 
 def joined(even, odd):
@@ -179,18 +204,15 @@
     att_v,
     b_src,
     b_dst,
+    z_src,
+    z_dst,
     c1_src,
     c1_dst,
-    c2_src,
     c2_dst,
     n_src,
     n_dst,
-    s_src,
-    s_dst,
-    e2_src,
-    e2_dst,
-    e3_src,
-    e3_dst,
+    e_src,
+    e_dst,
     g_src,
     g_dst,
     load_sem,
@@ -198,18 +220,16 @@
     page_sem,
     bs,
     br,
+    zs,
+    zr,
     c1s,
     c1r,
     c2s,
     c2r,
     ns,
     nr,
-    ss,
-    sr,
-    e2s,
-    e2r,
-    e3s,
-    e3r,
+    es,
+    er,
     gs,
     gr,
 ):
@@ -222,13 +242,18 @@
         return copy
 
     in_at = pl.multiple_of(gx * LOCAL_IN, LOCAL_IN)
-    head_at = pl.multiple_of(gx * HEAD_DIM, HEAD_DIM)
+    core = lax.rem(gx, 2)
+    partner = gx + 1 - 2 * core
+    z = lax.div(gx, 2)
+    heads_at = pl.multiple_of(core * HALF, HALF)
     loads = [
         load(0, hidden, hid_v),
         load(1, gain.at[pl.ds(pl.multiple_of(gx * 16, 16), 16), :], gain_v),
         load(2, consts, const_v),
+        load(4, q_down, qd_v),
+        load(6, kv_codes, kc_v),
+        load(7, kv_absmax, ka_v),
         load(3, q_absmax, qa_v),
-        load(4, q_down, qd_v),
         load(5, q_up, qu_v),
     ]
     q_loads = []
@@ -237,9 +262,7 @@
         q_loads.append(pltpu.make_async_copy(q_codes.at[part, :], qc_v.at[part, :], code_sem.at[c]))
         q_loads[-1].start()
     later = [
-        load(6, kv_codes, kc_v),
-        load(7, kv_absmax, ka_v),
-        load(8, q_magnitude.at[:, pl.ds(head_at, HEAD_DIM)], qm_v),
+        load(8, q_magnitude.at[:, pl.ds(heads_at, HALF)], qm_v),
         load(9, pages, pt_v),
     ]
     o_small = [load(10, o_absmax, oa_v), load(11, o_down, od_v), load(12, o_up, ou_v), load(13, o_magnitude, om_v)]
@@ -265,6 +288,16 @@
             barrier, inc=1, device_id={"gy": lax.rem(gy + k, NY)}, device_id_type=MESH
         )
 
+    def to_partner(src, dst, send, recv):
+        return pltpu.make_async_remote_copy(
+            src_ref=src,
+            dst_ref=dst,
+            send_sem=send.at[0],
+            recv_sem=recv.at[0],
+            device_id={"gx": partner},
+            device_id_type=MESH,
+        )
+
     def to_gx(k, src, dst, send, recv):
         return pltpu.make_async_remote_copy(
             src_ref=src,
@@ -287,9 +320,6 @@
 
     started = []
 
-    for copy in loads:
-        copy.wait()
-
     row8 = rows_of((ROWS, 128))
     lane8 = lanes_of((ROWS, 128))
     tenant_of = jnp.zeros((ROWS, 128), jnp.int32)
@@ -297,7 +327,9 @@
     for r in range(ROWS):
         tenant_of = jnp.where(row8 == r, tenant[r], tenant_of)
         length_of = jnp.where(row8 == r, lengths[r], length_of)
-    angles = length_of.astype(F32) * const_v[8:16, :]
+    for copy in loads[0:3]:
+        copy.wait()
+    angles = length_of.astype(F32) * const_v[16:24, :]
     cosine = jnp.cos(angles)
     sine = jnp.sin(angles)
     sine = jnp.where(lane8 < 64, -sine, sine)
@@ -320,10 +352,13 @@
         normed.append(x)
     normed = jnp.concatenate(normed, axis=1)
     lhs_v[0:16, :] = jnp.concatenate([normed, jnp.zeros_like(normed)], axis=0).astype(BF16)
+    for copy in loads[3:]:
+        copy.wait()
     lhs_v[16:144, :] = qd_v[...]
 
     lane64 = lanes_of((64, 128))
-    table = jnp.broadcast_to(const_v[0:1, :], (64, 128))
+    tables = (const_v[0:8, :], const_v[8:16, :])
+    parting = even_first()
 
     def dequantize(codes, row, scale_row):
         for c in range(4):
@@ -331,7 +366,7 @@
             words = codes[pl.ds(row, 64), cols]
             for half, (scales, ref) in enumerate(((ae_v, we_v), (ao_v, wo_v))):
                 code = words & 15 if half == 0 else words >> 4
-                value = lookup(table, code) * scales[c, pl.ds(scale_row, 1), :]
+                value = levels(tables, code) * scales[c, pl.ds(scale_row, 1), :]
                 ref[pl.ds(row, 64), cols] = value.astype(BF16)
                 square = value * value
                 part = square[0:8]
@@ -339,28 +374,33 @@
                     part = part + square[8 * j : 8 * j + 8]
                 sq_v[half, :, cols] += part
 
+    def weight_chunk(codes, c, lhs_rows):
+        base = c * CHUNK if isinstance(c, int) else pl.multiple_of(c * CHUNK, CHUNK)
+        for b in range(CHUNK // QBLOCK):
+            row = c * CHUNK + b * QBLOCK
+            row = row if isinstance(c, int) else pl.multiple_of(row, QBLOCK)
+            dequantize(codes, row, c * (CHUNK // QBLOCK) + b)
+        left = lhs_v[lhs_rows, pl.ds(base, CHUNK)]
+        acc_v[0, lhs_rows, :] += dot(left, we_v[pl.ds(base, CHUNK), :])
+        acc_v[1, lhs_rows, :] += dot(left, wo_v[pl.ds(base, CHUNK), :])
+
     def weight_chunks(codes, first, last, lhs_rows):
-        def chunk(c, carry):
-            base = pl.multiple_of(c * CHUNK, CHUNK)
-            for b in range(CHUNK // QBLOCK):
-                row = pl.multiple_of(c * CHUNK + b * QBLOCK, QBLOCK)
-                dequantize(codes, row, c * (CHUNK // QBLOCK) + b)
-            left = lhs_v[lhs_rows, pl.ds(base, CHUNK)]
-            acc_v[0, lhs_rows, :] += dot(left, we_v[pl.ds(base, CHUNK), :])
-            acc_v[1, lhs_rows, :] += dot(left, wo_v[pl.ds(base, CHUNK), :])
+        def step(c, carry):
+            weight_chunk(codes, c, lhs_rows)
             return carry
 
-        lax.fori_loop(first, last, chunk, 0)
+        lax.fori_loop(first, last, step, 0)
 
     def begin_projection(absmax, up):
-        even, odd = parted(absmax[...])
         for c in range(4):
-            ae_v[c] = even[:, 128 * c : 128 * c + 128]
-            ao_v[c] = odd[:, 128 * c : 128 * c + 128]
-        for c in range(4):
-            even, odd = parted(up[:, 256 * c : 256 * c + 256].astype(F32))
-            up_v[0, :, 128 * c : 128 * c + 128] = even.astype(BF16)
-            up_v[1, :, 128 * c : 128 * c + 128] = odd.astype(BF16)
+            part = slice(256 * c, 256 * c + 256)
+            parts = dot(jnp.concatenate(three_parts(absmax[:, part]), axis=0), parting)
+            whole = parts[0:32] + parts[32:64] + parts[64:96]
+            ae_v[c] = whole[:, 0:128]
+            ao_v[c] = whole[:, 128:256]
+            both = dot(up[:, part], parting).astype(BF16)
+            up_v[0, :, 128 * c : 128 * c + 128] = both[:, 0:128]
+            up_v[1, :, 128 * c : 128 * c + 128] = both[:, 128:256]
         acc_v[...] = jnp.zeros_like(acc_v)
         sq_v[...] = jnp.zeros_like(sq_v)
 
@@ -391,8 +431,6 @@
         return halves
 
     begin_projection(qa_v, qu_v)
-    for copy in later:
-        copy.wait()
 
     lane32 = lanes_of((32, 128))
     at = jnp.where(lane32 < 64, 2 * lane32, 2 * lane32 - 127)
@@ -405,7 +443,7 @@
             code = words & 15 if half == 0 else words >> 4
             scale = lookup(kv_scale[64 * half : 64 * half + 64], 2 * c + (lane64 >> 6))
             kvw_v[64 * half : 64 * half + 64, c * 128 : (c + 1) * 128] = (
-                lookup(table, code) * scale
+                levels(tables, code) * scale
             ).astype(BF16)
     keyval = dot_nt(lhs_v[0:16, :], kvw_v[...])[0:8]
     keyval = lookup(keyval, jnp.where((lane8 & 1) == 0, lane8 >> 1, 64 + (lane8 >> 1)))
@@ -413,69 +451,69 @@
     inner = dot_nt(lhs_v[...], lhs_v[16:144, :])
     middle, gram = inner[0:8], inner[16:144]
 
-    for copy in q_loads:
-        copy.wait()
-    weight_chunks(qc_v, 0, CHUNKS, slice(0, 144))
+    for c in range(CHUNKS):
+        q_loads[c].wait()
+        weight_chunk(qc_v, c, slice(0, 144))
 
     extra = adapter(middle)
     product = joined(acc_v[0, 0:8, :] + extra[0], acc_v[1, 0:8, :] + extra[1])
     norms = joined(*norm_parts(gram))
-    for i in range(NX):
-        b_src[i, 0] = product[i]
-        b_src[i, 1] = norms[i]
-        b_src[i, 2] = keyval
+    for half in range(2):
+        for m in range(4):
+            b_src[half, m] = product[4 * half + m]
+            b_src[half, 4 + m] = norms[4 * half + m]
+        b_src[half, 8] = keyval
 
     pl.semaphore_wait(barrier, NX - 1 + NY - 1)
 
-    b_copies = []
-    for k in range(1, NX):
-        peer = lax.rem(gx + k, NX)
-        b_copies.append(to_gx(k, b_src.at[peer], b_dst.at[k], bs, br))
-        b_copies[-1].start()
-    started += b_copies
-
+    b_copy = to_partner(b_src.at[1 - core], b_dst, bs, br)
+    b_copy.start()
+    started.append(b_copy)
     for copy in o_small:
         copy.wait()
+    lhs_v[16:144, :] = od_v[...]
+    o_gram = dot_nt(lhs_v[16:144, :], lhs_v[16:144, :])
+    b_copy.wait_recv()
+    z_src[...] = b_src[core] + b_dst[...]
+    z_dst[z] = z_src[...]
+    z_copies = []
+    for k in range(1, 4):
+        z_copies.append(to_gx(2 * k, z_src, z_dst.at[z], zs, zr))
+        z_copies[-1].start()
+    started += z_copies
+
+    begin_projection(oa_v, ou_v)
     for copy in o_loads:
         copy.wait()
-    begin_projection(oa_v, ou_v)
-    lhs_v[16:144, :] = od_v[...]
-    o_gram = dot_nt(lhs_v[16:144, :], lhs_v[16:144, :])
     down_rows = slice(16, 144)
-    weight_chunks(oc_v, 0, 2, down_rows)
-
-    summed = [b_src[gx, j] for j in range(3)]
-    for copy in b_copies:
+    weight_chunks(oc_v, 0, 3, down_rows)
+
+    for copy in later:
+        copy.wait()
+    for copy in z_copies:
         copy.wait_recv()
-    for k in range(1, NX):
-        for j in range(3):
-            summed[j] = summed[j] + b_dst[k, j]
-    magnitude = jnp.zeros((ROWS, 128), F32)
-    for t in range(TENANTS):
-        magnitude = jnp.where(tenant_of == t, qm_v[t : t + 1, :], magnitude)
-    query = rope(summed[0] * (magnitude * lax.rsqrt(summed[1])))
-    new = jnp.where(gy < KV_HEADS, rope(summed[2]), summed[2])
-    c1_src[...] = jnp.concatenate([query, new], axis=0).astype(BF16)
+    summed = z_dst[0]
+    for k in range(1, 4):
+        summed = summed + z_dst[k]
+    queries = []
+    for m in range(4):
+        magnitude = jnp.zeros((ROWS, 128), F32)
+        for t in range(TENANTS):
+            magnitude = jnp.where(
+                tenant_of == t, qm_v[t : t + 1, 128 * m : 128 * m + 128], magnitude
+            )
+        queries.append(rope(summed[m] * (magnitude * lax.rsqrt(summed[4 + m]))))
+    new = jnp.where(gy < KV_HEADS, rope(summed[8]), summed[8])
+    c1_src[0:16, :] = jnp.concatenate(queries[0:2], axis=0).astype(BF16)
+    c1_src[16:32, :] = jnp.concatenate(queries[2:4], axis=0).astype(BF16)
+    c1_src[32:48, :] = jnp.concatenate([new, jnp.zeros_like(new)], axis=0).astype(BF16)
     c1_dst[gy] = c1_src[...]
     c1_copies = []
     for k in range(1, NY):
         c1_copies.append(to_gy(k, c1_src, c1_dst.at[gy], c1s, c1r))
         c1_copies[-1].start()
     started += c1_copies
-    weight_chunks(oc_v, 2, 4, down_rows)
-
-    for copy in c1_copies:
-        copy.wait_recv()
-    for j in range(NY // 2):
-        pair = [c1_dst[2 * j + n].astype(F32)[0:8] for n in range(2)]
-        c2_src[16 * j : 16 * j + 16, :] = jnp.concatenate(pair, axis=0).astype(BF16)
-    c2_dst[gx] = c2_src[...]
-    c2_copies = []
-    for k in range(1, NX):
-        c2_copies.append(to_gx(k, c2_src, c2_dst.at[gx], c2s, c2r))
-        c2_copies[-1].start()
-    started += c2_copies
-    weight_chunks(oc_v, 4, CHUNKS, down_rows)
+    weight_chunks(oc_v, 3, CHUNKS, down_rows)
     o_norms = joined(*norm_parts(o_gram))
     for i in range(8):
         flat_v[8 * i : 8 * i + 8, :] = o_norms[i]
@@ -501,12 +539,20 @@
     def same(a, b):
         return jnp.where(a == b, 1.0, 0.0).astype(F32)
 
-    for copy in c2_copies:
+    for copy in c1_copies:
         copy.wait_recv()
-    for i in range(NX):
-        block = c2_dst[i].astype(F32)
-        for j in range(NY):
-            qf_v[pl.ds(8 * j + i, 8, stride=HEADS), :] = block[8 * j : 8 * j + 8]
+    c2_copy = to_partner(c1_dst.at[:, 0:32, :], c2_dst, c2s, c2r)
+    c2_copy.start()
+    started.append(c2_copy)
+    for j in range(NY):
+        block = c1_dst[j].astype(F32)
+        for m in range(4):
+            qf_v[pl.ds(8 * j + 4 * core + m, 8, stride=HEADS), :] = block[8 * m : 8 * m + 8]
+    c2_copy.wait_recv()
+    for j in range(NY):
+        block = c2_dst[j].astype(F32)
+        for m in range(4):
+            qf_v[pl.ds(8 * j + 4 - 4 * core + m, 8, stride=HEADS), :] = block[8 * m : 8 * m + 8]
 
     even_group = ((rows_of((HEADS, 128)) >> 4) & 1) == 0
     token = lanes_of((HEADS, PAGE)).astype(F32)
@@ -554,85 +600,106 @@
         nbf_v[pl.ds(r, HEADS, stride=ROWS), :] = number
         stats = jnp.where(lane_h == r, peak, stats)
         stats = jnp.where(lane_h == 8 + r, total, stats)
-    s_src[...] = stats.T[0:16]
-    n_src[...] = nbf_v[...].astype(BF16)
+    stats = three_parts(stats.T[0:16])
+    stats = [x.astype(F32) for x in stats]
+    lane16 = lanes_of((16, 128))
+    for i in range(NX):
+        n_src[i, 0:128, :] = nbf_v[128 * i : 128 * i + 128, :].astype(BF16)
+        mine = [pltpu.roll(x, (16 * n - 16 * i) % 128, 1) if (n - i) % 8 else x for n, x in enumerate(stats)]
+        n_src[i, 128:144, :] = jnp.where(
+            lane16 < 16, mine[0], jnp.where(lane16 < 32, mine[1], mine[2])
+        ).astype(BF16)
 
     n_copies = []
     for k in range(1, NX):
         peer = lax.rem(gx + k, NX)
-        part = pl.ds(pl.multiple_of(peer * 128, 128), 128)
-        n_copies.append(to_gx(k, s_src, s_dst.at[k], ss, sr))
-        n_copies[-1].start()
-        n_copies.append(to_gx(k, n_src.at[part, :], n_dst.at[k], ns, nr))
+        n_copies.append(to_gx(k, n_src.at[peer], n_dst.at[k], ns, nr))
         n_copies[-1].start()
     started += n_copies
 
-    own_q = qf_v[pl.ds(16 * gx + gy, 8, stride=HEADS), :]
-    new_key = c1_dst[gx].astype(F32)[8:16]
-    new_value = c1_dst[KV_HEADS + gx].astype(F32)[8:16]
-    self_score = jnp.sum(own_q * new_key, axis=1, keepdims=True) * INV_ROOT
+    new_key = c1_dst[gx].astype(F32)[32:40]
+    new_value = c1_dst[KV_HEADS + gx].astype(F32)[32:40]
+    self_score = jnp.zeros((ROWS, 128), F32)
+    for h in range(16):
+        q = qf_v[pl.ds(16 * gx + h, 8, stride=HEADS), :]
+        score = jnp.sum(q * new_key, axis=1, keepdims=True) * INV_ROOT
+        self_score = jnp.where(lane8 == h, score, self_score)
+
+    states = hid_v[:, pl.ds(pl.multiple_of(gy * 1024, 1024), 1024)].astype(F32)
+    mine = tenant[gx]
+    out_magnitude = jnp.zeros((8, 128), F32)
+    for i in range(8):
+        flat_v[8 * i : 8 * i + 8, :] = om_v[:, 128 * i : 128 * i + 128]
+    for t in range(TENANTS):
+        out_magnitude = jnp.where(mine == t, flat_v[pl.ds(t, 8, stride=8), :], out_magnitude)
+    for i in range(8):
+        flat_v[8 * i : 8 * i + 8, :] = states[:, 128 * i : 128 * i + 128]
+    residual = flat_v[pl.ds(gx, 8, stride=8), :]
+
+    def gathered(x, first):
+        parts = [pltpu.roll(x, 128 - first - 16 * n, 1) if first + n else x for n in range(3)]
+        return parts[0] + parts[1] + parts[2]
 
     for copy in n_copies:
         copy.wait_recv()
-    n_dst[0] = n_src[pl.ds(pl.multiple_of(gx * 128, 128), 128), :]
-    s_dst[0] = s_src[...]
-    peak = s_dst[0, 0:8]
+    n_dst[0] = n_src[gx]
+    seen = [gathered(n_dst[k, 128:144, :].astype(F32), 0) for k in range(NX)]
+    peak = seen[0][0:8]
     for k in range(1, NX):
-        peak = jnp.maximum(peak, s_dst[k, 0:8])
+        peak = jnp.maximum(peak, seen[k][0:8])
     total = jnp.zeros((ROWS, 128), F32)
-    shift = lax.rem(128 - 16 * gx, 128)
     factors = []
     for k in range(NX):
-        factor = jnp.exp(s_dst[k, 0:8] - peak)
-        total = total + factor * s_dst[k, 8:16]
-        factors.append(pltpu.roll(factor, shift, 1))
-    peak = pltpu.roll(peak, shift, 1)
-    total = pltpu.roll(total, shift, 1)
-    for j in range(NY // 2):
+        factors.append(jnp.exp(seen[k][0:8] - peak))
+        total = total + factors[k] * seen[k][8:16]
+    for j in range(8):
         pair = [jnp.zeros((ROWS, 128), F32), jnp.zeros((ROWS, 128), F32)]
         for k in range(NX):
             block = n_dst[k, 16 * j : 16 * j + 16, :].astype(F32)
             for n in range(2):
                 h = 2 * j + n
                 pair[n] = pair[n] + block[8 * n : 8 * n + 8] * factors[k][:, h : h + 1]
+        e_src[16 * j : 16 * j + 16, :] = jnp.concatenate(pair, axis=0).astype(BF16)
+    stats = jnp.zeros((ROWS, 128), F32)
+    for n, x in enumerate(three_parts(peak) + three_parts(total)):
+        x = x.astype(F32)
+        x = pltpu.roll(x, 16 * n, 1) if n else x
+        stats = jnp.where(jnp.logical_and(lane8 >= 16 * n, lane8 < 16 * n + 16), x, stats)
+    e_src[128:144, :] = jnp.concatenate([stats, jnp.zeros_like(stats)], axis=0).astype(BF16)
+
+    e_dst[gy] = e_src[...]
+    e_copies = []
+    for k in range(1, NY):
+        e_copies.append(to_gy(k, e_src, e_dst.at[gy], es, er))
+        e_copies[-1].start()
+    started += e_copies
+    for copy in e_copies:
+        copy.wait_recv()
+    peaks, totals = [], []
+    peak = self_score
+    for k in range(NY):
+        x = e_dst[k, 128:144, :].astype(F32)[0:8]
+        peaks.append(gathered(x, 0))
+        totals.append(gathered(x, 48))
+        peak = jnp.maximum(peak, peaks[k])
+    own = jnp.exp(self_score - peak)
+    total = own
+    factors = []
+    for k in range(NY):
+        factors.append(jnp.exp(peaks[k] - peak))
+        total = total + factors[k] * totals[k]
+    for j in range(8):
+        pair = [own[:, 2 * j + n : 2 * j + n + 1] * new_value for n in range(2)]
+        for k in range(NY):
+            block = e_dst[k, 16 * j : 16 * j + 16, :].astype(F32)
+            for n in range(2):
+                h = 2 * j + n
+                pair[n] = pair[n] + block[8 * n : 8 * n + 8] * factors[k][:, h : h + 1]
         for n in range(2):
             h = 2 * j + n
-            e2_src[h, 0] = pair[n]
-            e2_src[h, 1] = jnp.where(lane8 < 64, peak[:, h : h + 1], total[:, h : h + 1])
-
-    e2_copies = []
-    for k in range(1, NY):
-        peer = lax.rem(gy + k, NY)
-        e2_copies.append(to_gy(k, e2_src.at[peer], e2_dst.at[k], e2s, e2r))
-        e2_copies[-1].start()
-    started += e2_copies
-    for copy in e2_copies:
-        copy.wait_recv()
-    e2_dst[0] = e2_src[gy]
-    peak = self_score
-    for k in range(NY):
-        peak = jnp.maximum(peak, e2_dst[k, 1][:, 0:1])
-    own = jnp.exp(self_score - peak)
-    number = own * new_value
-    total = own
-    for k in range(NY):
-        both = e2_dst[k, 1]
-        factor = jnp.exp(both[:, 0:1] - peak)
-        number = number + factor * e2_dst[k, 0]
-        total = total + factor * both[:, 64:65]
-    e3_src[...] = (number / total).astype(BF16).astype(F32)
-    e3_dst[gy] = e3_src[...]
-    e3_copies = []
-    for k in range(1, NY):
-        e3_copies.append(to_gy(k, e3_src, e3_dst.at[gy], e3s, e3r))
-        e3_copies[-1].start()
-    started += e3_copies
-    for copy in e3_copies:
-        copy.wait_recv()
-
-    for j in range(NY):
-        x = e3_dst[j]
-        att_v[:, 128 * j : 128 * j + 128] = jnp.concatenate([x, jnp.zeros_like(x)], axis=0).astype(BF16)
+            x = pair[n] / total[:, h : h + 1]
+            att_v[:, 128 * h : 128 * h + 128] = jnp.concatenate([x, jnp.zeros_like(x)], axis=0).astype(BF16)
+
     attended = att_v[...]
     middle = dot_nt(attended, lhs_v[16:144, :])[0:8]
     extra = adapter(middle)
@@ -650,23 +717,14 @@
         g_copies[-1].start()
     started += g_copies
 
-    states = hid_v[:, pl.ds(pl.multiple_of(gy * 1024, 1024), 1024)].astype(F32)
-    mine = tenant[gx]
-    magnitude = jnp.zeros((8, 128), F32)
-    for i in range(8):
-        flat_v[8 * i : 8 * i + 8, :] = om_v[:, 128 * i : 128 * i + 128]
-    for t in range(TENANTS):
-        magnitude = jnp.where(mine == t, flat_v[pl.ds(t, 8, stride=8), :], magnitude)
-    for i in range(8):
-        flat_v[8 * i : 8 * i + 8, :] = states[:, 128 * i : 128 * i + 128]
-    residual = flat_v[pl.ds(gx, 8, stride=8), :]
     summed = [g_src[gx, j] for j in range(2)]
     for copy in g_copies:
         copy.wait_recv()
     for k in range(1, NX):
         for j in range(2):
             summed[j] = summed[j] + g_dst[k, j]
-    out[...] = residual + summed[0] * (magnitude * lax.rsqrt(summed[1]))
+    result = (residual + summed[0] * (out_magnitude * lax.rsqrt(summed[1]))).astype(BF16)
+    out[...] = result
     for copy in started:
         copy.wait_send()
 
@@ -712,13 +770,13 @@
         vmem((32, 1024), F32),
         vmem((128, LOCAL_IN), BF16),
         vmem((128, 1024), BF16),
-        vmem((8, 128), F32),
+        vmem((8, HALF), F32),
         vmem((128, LOCAL_IN), BF16),
         vmem((128, 1024), BF16),
         vmem((8, 1024), F32),
         vmem((8, 96), jnp.int32),
         vmem((SLOTS, 2, PAGE, 1024), BF16),
-        vmem((16, 128), F32),
+        vmem((24, 128), F32),
         vmem((4, 32, 128), F32),
         vmem((4, 32, 128), F32),
         vmem((2, 128, HALF), BF16),
@@ -734,37 +792,32 @@
         vmem((SLOTS, HEADS, HEAD_DIM), F32),
         vmem((ROWS * HEADS, HEAD_DIM), F32),
         vmem((16, LOCAL_IN), BF16),
-        vmem((NX, 3, 8, 128), F32),
-        vmem((NX, 3, 8, 128), F32),
-        vmem((16, 128), BF16),
-        vmem((NY, 16, 128), BF16),
-        vmem((128, 128), BF16),
-        vmem((NX, 128, 128), BF16),
-        vmem((ROWS * HEADS, HEAD_DIM), BF16),
-        vmem((NX, 128, 128), BF16),
-        vmem((16, 128), F32),
-        vmem((NX, 16, 128), F32),
-        vmem((NY, 2, 8, 128), F32),
-        vmem((NY, 2, 8, 128), F32),
-        vmem((8, 128), F32),
-        vmem((NY, 8, 128), F32),
+        vmem((2, 9, 8, 128), F32),
+        vmem((9, 8, 128), F32),
+        vmem((9, 8, 128), F32),
+        vmem((4, 9, 8, 128), F32),
+        vmem((48, 128), BF16),
+        vmem((NY, 48, 128), BF16),
+        vmem((NY, 32, 128), BF16),
+        vmem((NX, 144, 128), BF16),
+        vmem((NX, 144, 128), BF16),
+        vmem((144, 128), BF16),
+        vmem((NY, 144, 128), BF16),
         vmem((NX, 2, 8, 128), F32),
         vmem((NX, 2, 8, 128), F32),
         dma((14,)),
         dma((2 * CHUNKS,)),
         dma((SLOTS,)),
+        dma((1,)),
+        dma((1,)),
         dma((NX,)),
         dma((NX,)),
         dma((NY,)),
         dma((NY,)),
+        dma((1,)),
+        dma((1,)),
         dma((NX,)),
         dma((NX,)),
-        dma((NX,)),
-        dma((NX,)),
-        dma((NX,)),
-        dma((NX,)),
-        dma((NY,)),
-        dma((NY,)),
         dma((NY,)),
         dma((NY,)),
         dma((NX,)),
@@ -772,7 +825,7 @@
     ]
     result = pl.pallas_call(
         kernel,
-        out_shape=jax.ShapeDtypeStruct((8, 128), F32),
+        out_shape=jax.ShapeDtypeStruct((8, 128), BF16),
         in_specs=[smem, smem] + [hbm] * 17,
         out_specs=pl.BlockSpec(memory_space=pltpu.VMEM),
         scratch_shapes=scratch,
@@ -801,7 +854,7 @@
         kv_cache,
         jnp.asarray(constants()),
     )
-    return result.reshape(1, 1024).astype(BF16)
+    return result.reshape(1, 1024)
 
 
 def solution(mesh):

time: 61.2 us -> 54.2 us (0.89)
  Pallas kernels: 59.8 us -> 52.8 us
  other arithmetic: 0.69 us -> 0 us
  local copies, waits for them, and re-layouts: 0.6 us -> 1.28 us
    pallas_call x1, Pallas kernels: 59.8 us -> 52.8 us  [local(): pl.pallas_call(kernel, out_shape=jax.ShapeDtypeStruct((8, 128), BF16), in...]
    unnamed x1 -> x0, other arithmetic: 0.69 us -> none
    unnamed x1, local copies, waits for them, and re-layouts: 0.6 us -> 1.28 us
where the time goes in v2:
time: 54.2 us; the launch traced here: 54.1 us
  Pallas kernels  52.8 us (97%)
  local copies, waits for them, and re-layouts  1.28 us (2%)
    pallas_call x1, Pallas kernels, local(): pl.pallas_call(kernel, out_shape=jax.ShapeDtypeStruct((8, 128), BF16), in...  52.8 us
    unnamed x1, local copies, waits for them, and re-layouts  1.28 us

profile of v2, /device:TPU:1, one launch (start us, length us, event | category | flops | bytes accessed | tf_op | source)
XLA Modules:
  0.0 54.1 jit_solution(2014731987525906736)
XLA Ops:
  0.0 52.8 %layer.1 = bf16[8,128]{1,0:T(8,128)(2,1)} custom-call(s32[8]{0:T(128)} %tenant.1, s32[8]{0:T(128)} %lengths.1, bf16[8,16384]{1,0:T(8,128)(2,1)} %hidden.1, f32[128,128]{1,0:T(8,128)} %bitcast.20, s32[2048,512]{1,0:T(8,128)} %q_codes.1, f32[32,1024]{1,0:T(8,128)} %q_absmax.1, s32[64,2048]{1,0:T(8,128)} %bitcast.15, f32[32,128]{1,0:T(8,128)} %kv_absmax.1, ...), custom_call_target="tpu_custom_call" | custom-call | tf_op jit(solution)/shard_map/layer/pallas_call | solution.py:826
  52.8 1.3 %copy.22 = bf16[1,1,8,128]{3,1,2,0:T(2,128)(2,1)} copy(bf16[1,1,8,128]{3,2,1,0:T(8,128)(2,1)} %bitcast.21) | data formatting | bytes 4096

commit v3 on v2

--- a/solution.py
+++ b/solution.py
@@ -24,6 +24,8 @@
 HALF = 512
 CHUNK = 256
 CHUNKS = LOCAL_IN // CHUNK
+LATER = 5
+FIRST = 2
 D = 16384
 
 NF4_LEVELS = (
@@ -209,6 +211,10 @@
     c1_src,
     c1_dst,
     c2_dst,
+    kv_src,
+    kv_dst,
+    new_src,
+    new_dst,
     n_src,
     n_dst,
     e_src,
@@ -226,6 +232,10 @@
     c1r,
     c2s,
     c2r,
+    ks,
+    kr,
+    news,
+    newr,
     ns,
     nr,
     es,
@@ -251,8 +261,6 @@
         load(1, gain.at[pl.ds(pl.multiple_of(gx * 16, 16), 16), :], gain_v),
         load(2, consts, const_v),
         load(4, q_down, qd_v),
-        load(6, kv_codes, kc_v),
-        load(7, kv_absmax, ka_v),
         load(3, q_absmax, qa_v),
         load(5, q_up, qu_v),
     ]
@@ -261,23 +269,6 @@
         part = pl.ds(c * CHUNK, CHUNK)
         q_loads.append(pltpu.make_async_copy(q_codes.at[part, :], qc_v.at[part, :], code_sem.at[c]))
         q_loads[-1].start()
-    later = [
-        load(8, q_magnitude.at[:, pl.ds(heads_at, HALF)], qm_v),
-        load(9, pages, pt_v),
-    ]
-    o_small = [load(10, o_absmax, oa_v), load(11, o_down, od_v), load(12, o_up, ou_v), load(13, o_magnitude, om_v)]
-    o_loads = []
-    for c in range(CHUNKS):
-        part = pl.ds(c * CHUNK, CHUNK)
-        o_loads.append(
-            pltpu.make_async_copy(o_codes.at[part, :], oc_v.at[part, :], code_sem.at[CHUNKS + c])
-        )
-        o_loads[-1].start()
-    page_loads = []
-    for s in range(SLOTS):
-        page_loads.append(pltpu.make_async_copy(cache.at[s], cache_v.at[s], page_sem.at[s]))
-        page_loads[-1].start()
-
     barrier = pltpu.get_barrier_semaphore()
     for k in range(1, NX):
         pl.semaphore_signal(
@@ -375,21 +366,12 @@
                 sq_v[half, :, cols] += part
 
     def weight_chunk(codes, c, lhs_rows):
-        base = c * CHUNK if isinstance(c, int) else pl.multiple_of(c * CHUNK, CHUNK)
+        base = c * CHUNK
         for b in range(CHUNK // QBLOCK):
-            row = c * CHUNK + b * QBLOCK
-            row = row if isinstance(c, int) else pl.multiple_of(row, QBLOCK)
-            dequantize(codes, row, c * (CHUNK // QBLOCK) + b)
+            dequantize(codes, base + b * QBLOCK, c * (CHUNK // QBLOCK) + b)
         left = lhs_v[lhs_rows, pl.ds(base, CHUNK)]
         acc_v[0, lhs_rows, :] += dot(left, we_v[pl.ds(base, CHUNK), :])
         acc_v[1, lhs_rows, :] += dot(left, wo_v[pl.ds(base, CHUNK), :])
-
-    def weight_chunks(codes, first, last, lhs_rows):
-        def step(c, carry):
-            weight_chunk(codes, c, lhs_rows)
-            return carry
-
-        lax.fori_loop(first, last, step, 0)
 
     def begin_projection(absmax, up):
         for c in range(4):
@@ -430,8 +412,59 @@
             halves.append(x[0:8] + x[8:16])
         return halves
 
+
     begin_projection(qa_v, qu_v)
 
+    inner = dot_nt(lhs_v[...], lhs_v[16:144, :])
+    middle, gram = inner[0:8], inner[16:144]
+
+    for c in range(CHUNKS):
+        q_loads[c].wait()
+        if c == LATER:
+            later = [
+                load(6, kv_codes, kc_v),
+                load(7, kv_absmax, ka_v),
+                load(8, q_magnitude.at[:, pl.ds(heads_at, HALF)], qm_v),
+                load(9, pages, pt_v),
+            ]
+            o_small = [load(10, o_absmax, oa_v), load(11, o_down, od_v), load(12, o_up, ou_v), load(13, o_magnitude, om_v)]
+            o_loads = [pltpu.make_async_copy(o_codes, oc_v, code_sem.at[CHUNKS])]
+            o_loads[0].start()
+            page_loads = []
+            for s in range(SLOTS):
+                page_loads.append(pltpu.make_async_copy(cache.at[s], cache_v.at[s], page_sem.at[s]))
+                page_loads[-1].start()
+
+        weight_chunk(qc_v, c, slice(0, 144))
+
+    extra = adapter(middle)
+    product = joined(acc_v[0, 0:8, :] + extra[0], acc_v[1, 0:8, :] + extra[1])
+    norms = joined(*norm_parts(gram))
+    for half in range(2):
+        for m in range(4):
+            b_src[half, m] = product[4 * half + m]
+            b_src[half, 4 + m] = norms[4 * half + m]
+
+    pl.semaphore_wait(barrier, NX - 1 + NY - 1)
+
+    b_copy = to_partner(b_src.at[1 - core], b_dst, bs, br)
+    b_copy.start()
+    started.append(b_copy)
+    for copy in o_small:
+        copy.wait()
+    lhs_v[16:144, :] = od_v[...]
+    o_gram = dot_nt(lhs_v[16:144, :], lhs_v[16:144, :])
+    b_copy.wait_recv()
+    z_src[...] = b_src[core] + b_dst[...]
+    z_dst[z] = z_src[...]
+    z_copies = []
+    for k in range(1, 4):
+        z_copies.append(to_gx(2 * k, z_src, z_dst.at[z], zs, zr))
+        z_copies[-1].start()
+    started += z_copies
+
+    for copy in later:
+        copy.wait()
     lane32 = lanes_of((32, 128))
     at = jnp.where(lane32 < 64, 2 * lane32, 2 * lane32 - 127)
     kv_scale = jnp.concatenate(
@@ -448,48 +481,19 @@
     keyval = dot_nt(lhs_v[0:16, :], kvw_v[...])[0:8]
     keyval = lookup(keyval, jnp.where((lane8 & 1) == 0, lane8 >> 1, 64 + (lane8 >> 1)))
 
-    inner = dot_nt(lhs_v[...], lhs_v[16:144, :])
-    middle, gram = inner[0:8], inner[16:144]
-
-    for c in range(CHUNKS):
-        q_loads[c].wait()
-        weight_chunk(qc_v, c, slice(0, 144))
-
-    extra = adapter(middle)
-    product = joined(acc_v[0, 0:8, :] + extra[0], acc_v[1, 0:8, :] + extra[1])
-    norms = joined(*norm_parts(gram))
-    for half in range(2):
-        for m in range(4):
-            b_src[half, m] = product[4 * half + m]
-            b_src[half, 4 + m] = norms[4 * half + m]
-        b_src[half, 8] = keyval
-
-    pl.semaphore_wait(barrier, NX - 1 + NY - 1)
-
-    b_copy = to_partner(b_src.at[1 - core], b_dst, bs, br)
-    b_copy.start()
-    started.append(b_copy)
-    for copy in o_small:
-        copy.wait()
-    lhs_v[16:144, :] = od_v[...]
-    o_gram = dot_nt(lhs_v[16:144, :], lhs_v[16:144, :])
-    b_copy.wait_recv()
-    z_src[...] = b_src[core] + b_dst[...]
-    z_dst[z] = z_src[...]
-    z_copies = []
-    for k in range(1, 4):
-        z_copies.append(to_gx(2 * k, z_src, z_dst.at[z], zs, zr))
-        z_copies[-1].start()
-    started += z_copies
-
+    kv_src[...] = keyval
+    kv_copies = []
+    for k in range(1, NX):
+        kv_copies.append(to_gx(k, kv_src, kv_dst.at[k], ks, kr))
+        kv_copies[-1].start()
+    started += kv_copies
     begin_projection(oa_v, ou_v)
     for copy in o_loads:
         copy.wait()
     down_rows = slice(16, 144)
-    weight_chunks(oc_v, 0, 3, down_rows)
-
-    for copy in later:
-        copy.wait()
+    for c in range(FIRST):
+        weight_chunk(oc_v, c, down_rows)
+
     for copy in z_copies:
         copy.wait_recv()
     summed = z_dst[0]
@@ -503,17 +507,29 @@
                 tenant_of == t, qm_v[t : t + 1, 128 * m : 128 * m + 128], magnitude
             )
         queries.append(rope(summed[m] * (magnitude * lax.rsqrt(summed[4 + m]))))
-    new = jnp.where(gy < KV_HEADS, rope(summed[8]), summed[8])
     c1_src[0:16, :] = jnp.concatenate(queries[0:2], axis=0).astype(BF16)
     c1_src[16:32, :] = jnp.concatenate(queries[2:4], axis=0).astype(BF16)
-    c1_src[32:48, :] = jnp.concatenate([new, jnp.zeros_like(new)], axis=0).astype(BF16)
     c1_dst[gy] = c1_src[...]
     c1_copies = []
     for k in range(1, NY):
         c1_copies.append(to_gy(k, c1_src, c1_dst.at[gy], c1s, c1r))
         c1_copies[-1].start()
     started += c1_copies
-    weight_chunks(oc_v, 3, CHUNKS, down_rows)
+    for copy in kv_copies:
+        copy.wait_recv()
+    new = kv_src[...]
+    for k in range(1, NX):
+        new = new + kv_dst[k]
+    new = jnp.where(gy < KV_HEADS, rope(new), new)
+    new_src[...] = jnp.concatenate([new, jnp.zeros_like(new)], axis=0).astype(BF16)
+    new_dst[gy] = new_src[...]
+    new_copies = []
+    for k in range(1, NY):
+        new_copies.append(to_gy(k, new_src, new_dst.at[gy], news, newr))
+        new_copies[-1].start()
+    started += new_copies
+    for c in range(FIRST, CHUNKS):
+        weight_chunk(oc_v, c, down_rows)
     o_norms = joined(*norm_parts(o_gram))
     for i in range(8):
         flat_v[8 * i : 8 * i + 8, :] = o_norms[i]
@@ -541,7 +557,7 @@
 
     for copy in c1_copies:
         copy.wait_recv()
-    c2_copy = to_partner(c1_dst.at[:, 0:32, :], c2_dst, c2s, c2r)
+    c2_copy = to_partner(c1_dst, c2_dst, c2s, c2r)
     c2_copy.start()
     started.append(c2_copy)
     for j in range(NY):
@@ -617,8 +633,10 @@
         n_copies[-1].start()
     started += n_copies
 
-    new_key = c1_dst[gx].astype(F32)[32:40]
-    new_value = c1_dst[KV_HEADS + gx].astype(F32)[32:40]
+    for copy in new_copies:
+        copy.wait_recv()
+    new_key = new_dst[gx].astype(F32)[0:8]
+    new_value = new_dst[KV_HEADS + gx].astype(F32)[0:8]
     self_score = jnp.zeros((ROWS, 128), F32)
     for h in range(16):
         q = qf_v[pl.ds(16 * gx + h, 8, stride=HEADS), :]
@@ -723,8 +741,9 @@
     for k in range(1, NX):
         for j in range(2):
             summed[j] = summed[j] + g_dst[k, j]
-    result = (residual + summed[0] * (out_magnitude * lax.rsqrt(summed[1]))).astype(BF16)
-    out[...] = result
+    result = (residual + summed[0] * (out_magnitude * lax.rsqrt(summed[1])))
+    for c in range(8):
+        out[0:1, 128 * c : 128 * c + 128] = result[c : c + 1, :]
     for copy in started:
         copy.wait_send()
 
@@ -792,13 +811,17 @@
         vmem((SLOTS, HEADS, HEAD_DIM), F32),
         vmem((ROWS * HEADS, HEAD_DIM), F32),
         vmem((16, LOCAL_IN), BF16),
-        vmem((2, 9, 8, 128), F32),
-        vmem((9, 8, 128), F32),
-        vmem((9, 8, 128), F32),
-        vmem((4, 9, 8, 128), F32),
-        vmem((48, 128), BF16),
-        vmem((NY, 48, 128), BF16),
+        vmem((2, 8, 8, 128), F32),
+        vmem((8, 8, 128), F32),
+        vmem((8, 8, 128), F32),
+        vmem((4, 8, 8, 128), F32),
+        vmem((32, 128), BF16),
         vmem((NY, 32, 128), BF16),
+        vmem((NY, 32, 128), BF16),
+        vmem((8, 128), F32),
+        vmem((NX, 8, 128), F32),
+        vmem((16, 128), BF16),
+        vmem((NY, 16, 128), BF16),
         vmem((NX, 144, 128), BF16),
         vmem((NX, 144, 128), BF16),
         vmem((144, 128), BF16),
@@ -806,7 +829,7 @@
         vmem((NX, 2, 8, 128), F32),
         vmem((NX, 2, 8, 128), F32),
         dma((14,)),
-        dma((2 * CHUNKS,)),
+        dma((CHUNKS + 1,)),
         dma((SLOTS,)),
         dma((1,)),
         dma((1,)),
@@ -822,10 +845,14 @@
         dma((NY,)),
         dma((NX,)),
         dma((NX,)),
+        dma((NY,)),
+        dma((NY,)),
+        dma((NX,)),
+        dma((NX,)),
     ]
     result = pl.pallas_call(
         kernel,
-        out_shape=jax.ShapeDtypeStruct((8, 128), BF16),
+        out_shape=jax.ShapeDtypeStruct((1, 1024), F32),
         in_specs=[smem, smem] + [hbm] * 17,
         out_specs=pl.BlockSpec(memory_space=pltpu.VMEM),
         scratch_shapes=scratch,
@@ -854,7 +881,7 @@
         kv_cache,
         jnp.asarray(constants()),
     )
-    return result.reshape(1, 1024)
+    return result.astype(BF16)
 
 
 def solution(mesh):

time: 54.2 us -> 53.4 us (0.985)
  other arithmetic: 0 us -> 1.28 us
  local copies, waits for them, and re-layouts: 1.28 us -> 0 us
  Pallas kernels: 52.8 us -> 51.9 us
    convert_element_type x0 -> x1, other arithmetic: none -> 1.28 us  [local(): return result.astype(BF16)]
    unnamed x1 -> x0, local copies, waits for them, and re-layouts: 1.28 us -> none
    pallas_call x1, Pallas kernels: 52.8 us -> 51.9 us  [local(): pl.pallas_call(kernel, out_shape=jax.ShapeDtypeStruct((1, 1024), F32), in...]
where the time goes in v3:
time: 53.4 us; the launch traced here: 53.2 us
  Pallas kernels  51.9 us (97%)
  other arithmetic  1.28 us (2%)
    pallas_call x1, Pallas kernels, local(): pl.pallas_call(kernel, out_shape=jax.ShapeDtypeStruct((1, 1024), F32), in...  51.9 us
    convert_element_type x1, other arithmetic, local(): return result.astype(BF16)  1.28 us

profile of v3, /device:TPU:1, one launch (start us, length us, event | category | flops | bytes accessed | tf_op | source)
XLA Modules:
  0.0 53.2 jit_solution(10841949681540107702)
XLA Ops:
  0.0 51.9 %layer.1 = f32[1,1024]{1,0:T(1,128)} custom-call(s32[8]{0:T(128)} %tenant.1, s32[8]{0:T(128)} %lengths.1, bf16[8,16384]{1,0:T(8,128)(2,1)} %hidden.1, f32[128,128]{1,0:T(8,128)} %bitcast.15, s32[2048,512]{1,0:T(8,128)} %q_codes.1, f32[32,1024]{1,0:T(8,128)} %q_absmax.1, s32[64,2048]{1,0:T(8,128)} %bitcast.10, f32[32,128]{1,0:T(8,128)} %kv_absmax.1, ...), custom_call_target="tpu_custom_call" | custom-call | tf_op jit(solution)/shard_map/layer/pallas_call | solution.py:853
  52.0 1.3 %convert_element_type.3 = bf16[1,1024]{1,0:T(2,128)(2,1)} convert(f32[1,1024]{1,0:T(1,128)} %layer.1) | non-fusion elementwise | flops 1024 | bytes 6144 | tf_op jit(solution)/shard_map/convert_element_type | solution.py:884

commit v4 on v3

--- a/solution.py
+++ b/solution.py
@@ -80,7 +80,7 @@
     )
 
 
-def levels(tables, code):
+def levels(tables, words, high):
     numbers = lax.GatherDimensionNumbers(
         offset_dims=(),
         collapsed_slice_dims=(0,),
@@ -99,10 +99,11 @@
         )
 
     parts = []
-    for j in range(code.shape[0] // 8):
-        part = code[8 * j : 8 * j + 8]
-        at = part & 7
-        parts.append(jnp.where((part & 8) != 0, pick(tables[1], at), pick(tables[0], at)))
+    for j in range(words.shape[0] // 8):
+        part = words[8 * j : 8 * j + 8]
+        at = (part >> 4 if high else part) & 7
+        upper = part > 127 if high else (part & 8) != 0
+        parts.append(jnp.where(upper, pick(tables[1], at), pick(tables[0], at)))
     return jnp.concatenate(parts, axis=0)
 
 
@@ -152,8 +153,8 @@
 
 
 def kernel(
-    tenant,
-    lengths,
+    tenant_h,
+    lengths_h,
     hidden,
     gain,
     q_codes,
@@ -172,6 +173,8 @@
     cache,
     consts,
     out,
+    tenant,
+    lengths,
     hid_v,
     gain_v,
     qc_v,
@@ -257,6 +260,8 @@
     z = lax.div(gx, 2)
     heads_at = pl.multiple_of(core * HALF, HALF)
     loads = [
+        load(14, tenant_h, tenant),
+        load(15, lengths_h, lengths),
         load(0, hidden, hid_v),
         load(1, gain.at[pl.ds(pl.multiple_of(gx * 16, 16), 16), :], gain_v),
         load(2, consts, const_v),
@@ -311,6 +316,9 @@
 
     started = []
 
+    for copy in loads[0:5]:
+        copy.wait()
+
     row8 = rows_of((ROWS, 128))
     lane8 = lanes_of((ROWS, 128))
     tenant_of = jnp.zeros((ROWS, 128), jnp.int32)
@@ -318,8 +326,6 @@
     for r in range(ROWS):
         tenant_of = jnp.where(row8 == r, tenant[r], tenant_of)
         length_of = jnp.where(row8 == r, lengths[r], length_of)
-    for copy in loads[0:3]:
-        copy.wait()
     angles = length_of.astype(F32) * const_v[16:24, :]
     cosine = jnp.cos(angles)
     sine = jnp.sin(angles)
@@ -343,7 +349,7 @@
         normed.append(x)
     normed = jnp.concatenate(normed, axis=1)
     lhs_v[0:16, :] = jnp.concatenate([normed, jnp.zeros_like(normed)], axis=0).astype(BF16)
-    for copy in loads[3:]:
+    for copy in loads[5:]:
         copy.wait()
     lhs_v[16:144, :] = qd_v[...]
 
@@ -356,8 +362,7 @@
             cols = slice(128 * c, 128 * c + 128)
             words = codes[pl.ds(row, 64), cols]
             for half, (scales, ref) in enumerate(((ae_v, we_v), (ao_v, wo_v))):
-                code = words & 15 if half == 0 else words >> 4
-                value = levels(tables, code) * scales[c, pl.ds(scale_row, 1), :]
+                value = levels(tables, words, half == 1) * scales[c, pl.ds(scale_row, 1), :]
                 ref[pl.ds(row, 64), cols] = value.astype(BF16)
                 square = value * value
                 part = square[0:8]
@@ -473,10 +478,9 @@
     for c in range(16):
         words = kc_v[:, c * 128 : (c + 1) * 128]
         for half in range(2):
-            code = words & 15 if half == 0 else words >> 4
             scale = lookup(kv_scale[64 * half : 64 * half + 64], 2 * c + (lane64 >> 6))
             kvw_v[64 * half : 64 * half + 64, c * 128 : (c + 1) * 128] = (
-                levels(tables, code) * scale
+                levels(tables, words, half == 1) * scale
             ).astype(BF16)
     keyval = dot_nt(lhs_v[0:16, :], kvw_v[...])[0:8]
     keyval = lookup(keyval, jnp.where((lane8 & 1) == 0, lane8 >> 1, 64 + (lane8 >> 1)))
@@ -777,8 +781,9 @@
     vmem = pltpu.VMEM
     dma = pltpu.SemaphoreType.DMA
     hbm = pl.BlockSpec(memory_space=pl.ANY)
-    smem = pl.BlockSpec(memory_space=pltpu.SMEM)
     scratch = [
+        pltpu.SMEM((8,), jnp.int32),
+        pltpu.SMEM((8,), jnp.int32),
         vmem((8, D), BF16),
         vmem((16, 128), F32),
         vmem((LOCAL_IN, HALF), jnp.int32),
@@ -828,7 +833,7 @@
         vmem((NY, 144, 128), BF16),
         vmem((NX, 2, 8, 128), F32),
         vmem((NX, 2, 8, 128), F32),
-        dma((14,)),
+        dma((16,)),
         dma((CHUNKS + 1,)),
         dma((SLOTS,)),
         dma((1,)),
@@ -853,7 +858,7 @@
     result = pl.pallas_call(
         kernel,
         out_shape=jax.ShapeDtypeStruct((1, 1024), F32),
-        in_specs=[smem, smem] + [hbm] * 17,
+        in_specs=[hbm] * 19,
         out_specs=pl.BlockSpec(memory_space=pltpu.VMEM),
         scratch_shapes=scratch,
         compiler_params=pltpu.CompilerParams(

time: 53.4 us -> 52.4 us (0.981)
  Pallas kernels: 51.9 us -> 51 us
    pallas_call x1, Pallas kernels: 51.9 us -> 51 us  [local(): pl.pallas_call(kernel, out_shape=jax.ShapeDtypeStruct((1, 1024), F32), in...]
where the time goes in v4:
time: 52.4 us; the launch traced here: 52.3 us
  Pallas kernels  51 us (97%)
  other arithmetic  1.28 us (2%)
    pallas_call x1, Pallas kernels, local(): pl.pallas_call(kernel, out_shape=jax.ShapeDtypeStruct((1, 1024), F32), in...  51 us
    convert_element_type x1, other arithmetic, local(): return result.astype(BF16)  1.28 us

profile of v4, /device:TPU:1, one launch (start us, length us, event | category | flops | bytes accessed | tf_op | source)
XLA Modules:
  0.0 52.3 jit_solution(7929855847947978579)
XLA Ops:
  0.0 51.0 %layer.1 = f32[1,1024]{1,0:T(1,128)} custom-call(s32[8]{0:T(128)} %tenant_h.1, s32[8]{0:T(128)} %lengths_h.1, bf16[8,16384]{1,0:T(8,128)(2,1)} %hidden.1, f32[128,128]{1,0:T(8,128)} %bitcast.15, s32[2048,512]{1,0:T(8,128)} %q_codes.1, f32[32,1024]{1,0:T(8,128)} %q_absmax.1, s32[64,2048]{1,0:T(8,128)} %bitcast.10, f32[32,128]{1,0:T(8,128)} %kv_absmax.1, ...), custom_call_target="tpu_custom_call" | custom-call | tf_op jit(solution)/shard_map/layer/pallas_call | solution.py:858
  51.0 1.3 %convert_element_type.3 = bf16[1,1024]{1,0:T(2,128)(2,1)} convert(f32[1,1024]{1,0:T(1,128)} %layer.1) | non-fusion elementwise | flops 1024 | bytes 6144 | tf_op jit(solution)/shard_map/convert_element_type | solution.py:889

commit v5 on v4

--- a/solution.py
+++ b/solution.py
@@ -22,10 +22,10 @@
 SLOTS = 5
 LOCAL_IN = 2048
 HALF = 512
-CHUNK = 256
+CHUNK = 512
 CHUNKS = LOCAL_IN // CHUNK
-LATER = 5
-FIRST = 2
+LATER = 2
+FIRST = 1
 D = 16384
 
 NF4_LEVELS = (

time: 52.4 us -> 51.5 us (0.983)
  Pallas kernels: 51 us -> 50.1 us
    pallas_call x1, Pallas kernels: 51 us -> 50.1 us  [local(): pl.pallas_call(kernel, out_shape=jax.ShapeDtypeStruct((1, 1024), F32), in...]
where the time goes in v5:
time: 51.5 us; the launch traced here: 51.4 us
  Pallas kernels  50.1 us (97%)
  other arithmetic  1.28 us (2%)
    pallas_call x1, Pallas kernels, local(): pl.pallas_call(kernel, out_shape=jax.ShapeDtypeStruct((1, 1024), F32), in...  50.1 us
    convert_element_type x1, other arithmetic, local(): return result.astype(BF16)  1.28 us

profile of v5, /device:TPU:1, one launch (start us, length us, event | category | flops | bytes accessed | tf_op | source)
XLA Modules:
  0.0 51.4 jit_solution(17909106530513429528)
XLA Ops:
  0.0 50.1 %layer.1 = f32[1,1024]{1,0:T(1,128)} custom-call(s32[8]{0:T(128)} %tenant_h.1, s32[8]{0:T(128)} %lengths_h.1, bf16[8,16384]{1,0:T(8,128)(2,1)} %hidden.1, f32[128,128]{1,0:T(8,128)} %bitcast.15, s32[2048,512]{1,0:T(8,128)} %q_codes.1, f32[32,1024]{1,0:T(8,128)} %q_absmax.1, s32[64,2048]{1,0:T(8,128)} %bitcast.10, f32[32,128]{1,0:T(8,128)} %kv_absmax.1, ...), custom_call_target="tpu_custom_call" | custom-call | tf_op jit(solution)/shard_map/layer/pallas_call | solution.py:858
  50.1 1.3 %convert_element_type.3 = bf16[1,1024]{1,0:T(2,128)(2,1)} convert(f32[1,1024]{1,0:T(1,128)} %layer.1) | non-fusion elementwise | flops 1024 | bytes 6144 | tf_op jit(solution)/shard_map/convert_element_type | solution.py:889
